TPU v7x, 32 devices: a whole 2x2x4 slice. The times are simulated.
32 devices in a mesh: seq: 8 (over y, x, core), chan: 4 (over z).
Axes of the slice: x: 2, y: 2, z: 4, core: 2. Of those that a mesh axis runs over, the one named last changes fastest.
Arguments:
- values_in: bfloat16 [4096, 1024], P(('seq', 'chan')), may hold values from -6 to 6
- gate_in: bfloat16 [4096, 1024], P(('seq', 'chan')), may hold values from -6 to 6
- gate_out: bfloat16 [4096, 1024], P(('seq', 'chan')), may hold values from -6 to 6
- cotangent: bfloat16 [4096, 1024], P(('seq', 'chan')), may hold values from -6 to 6
- filter_spectra: float32 [2, 8, 2, 512, 1024], P(None, 'seq', None, None, 'chan'), may hold values from -4 to 4, as said below
Outputs:
- output: bfloat16 [4096, 1024], P(('seq', 'chan'))
- grad_values: bfloat16 [4096, 1024], P(('seq', 'chan'))
- grad_gate_in: bfloat16 [4096, 1024], P(('seq', 'chan'))
- grad_gate_out: bfloat16 [4096, 1024], P(('seq', 'chan'))
- grad_filter: float32 [2, 8, 2, 512, 1024], P(None, 'seq', None, None, 'chan')
Inputs may be any that keep to these rules, and one draw needn't show every extreme that they name: `filter_spectra`: the spectrum is that of a real filter: the value at frequency 8192 - f is the complex conjugate of the value at f, and the values at frequencies 0 and 4096 are real.
All inputs are finite; a program needn't handle non-finite values.
Results may differ from a plain program's by a relative error of at most 0.001.
Values may be sent and summed in bfloat16 or wider, within the bound.
A program may use at most 128 MiB of HBM per device.

v0:
```python
import functools
import math

import jax
import jax.numpy as jnp
import numpy as np
from jax import lax
from jax.experimental import pallas as pl
from jax.experimental.pallas import tpu as pltpu
from jax.sharding import PartitionSpec as P

MESH = pl.DeviceIdType.MESH
ANY = pl.BlockSpec(memory_space=pl.ANY)
WHOLE = pl.BlockSpec(memory_space=pltpu.VMEM)


def mirrored(number, bits):
    out = 0
    for place in range(bits):
        out = out + ((number >> place) & 1) * (1 << (bits - 1 - place))
    return out


def meet(peers):
    barrier = pltpu.get_barrier_semaphore()
    for peer in peers:
        pl.semaphore_signal(barrier, inc=1, device_id=peer, device_id_type=MESH)
    pl.semaphore_wait(barrier, len(peers))


def gather_kernel(shards, groups, *refs):
    source, filt, held, other = refs[:4]
    own_sem, z_send, z_recv, s_send, s_recv, f_send, f_recv = refs[4:]
    s, c = lax.axis_index("seq"), lax.axis_index("chan")
    half = s % 2
    pair = s // 2
    lanes = source.shape[-1]
    bits = shards.bit_length() - 1
    near = [(d, e) for d in range(groups) for e in range(2) if d or e]
    meet([(s ^ e, c ^ d) for d, e in near] + [(s ^ (1 << b), c) for b in range(1, bits)])

    def cross(d, e, landing):
        return pltpu.make_async_remote_copy(
            src_ref=source.at[c ^ d, half ^ e],
            dst_ref=held.at[s ^ e, c ^ d] if landing else held.at[s, c],
            send_sem=z_send.at[d * 2 + e],
            recv_sem=z_recv.at[d * 2 + e],
            device_id=(s ^ e, c ^ d),
            device_id_type=MESH,
        )

    for d, e in near:
        cross(d, e, False).start()
    own = pltpu.make_async_copy(source.at[c, half], held.at[s, c], own_sem)
    own.start()
    swap = pltpu.make_async_remote_copy(
        src_ref=filt.at[:, :, :, :, pl.ds(pl.multiple_of((half ^ 1) * lanes, lanes), lanes)],
        dst_ref=other,
        send_sem=f_send,
        recv_sem=f_recv,
        device_id=(s ^ 1, c),
        device_id_type=MESH,
    )

    def piece(d, owner, slot, partner):
        place = held.at[pl.ds(owner * 2, 2), c ^ d]
        return pltpu.make_async_remote_copy(
            src_ref=place,
            dst_ref=place,
            send_sem=s_send.at[d * (shards // 2) + slot],
            recv_sem=s_recv.at[d * (shards // 2) + slot],
            device_id=(partner * 2 + half, c),
            device_id_type=MESH,
        )

    far = list(range(bits - 1))
    sent, landed = [], []
    for tick in range((groups + 1) // 2 * bits):
        for d in range(groups):
            order = far if d % 2 == 0 else far[::-1]
            depth = tick - d // 2 * bits
            for mask in range(shards // 2):
                if bin(mask).count("1") != depth:
                    continue
                last = max([order.index(b) for b in far if mask >> b & 1], default=-1)
                later = order[last + 1 :]
                if not later:
                    landed.append((d, mask))
                    continue
                if mask:
                    piece(d, pair ^ mask, mask, pair).wait_recv()
                else:
                    for e in range(2):
                        if d or e:
                            cross(d, e, True).wait_recv()
                        else:
                            own.wait()
                for b in later:
                    copy = piece(d, pair ^ mask, mask ^ (1 << b), pair ^ (1 << b))
                    copy.start()
                    sent.append(copy)
        if tick == 0:
            swap.start()
    for d, mask in landed:
        piece(d, pair ^ mask, mask, pair).wait_recv()
    swap.wait_recv()
    for d, e in near:
        cross(d, e, False).wait_send()
    for copy in sent:
        copy.wait_send()
    swap.wait_send()


def arrange_kernel(*refs):
    lanes = refs[4].shape[-1]
    for side in range(2):
        for a in range(4):
            refs[4][0, side, a] = refs[a][:, side * lanes : (side + 1) * lanes]


def arrange(inputs, groups):
    rows, channels = inputs[0].shape
    width = channels // groups
    lanes = width // 2
    return pl.pallas_call(
        arrange_kernel,
        grid=(groups,),
        out_shape=jax.ShapeDtypeStruct((groups, 2, 4, rows, lanes), inputs[0].dtype),
        in_specs=[pl.BlockSpec((rows, width), lambda n: (0, n))] * 4,
        out_specs=pl.BlockSpec((1, 2, 4, rows, lanes), lambda n: (n, 0, 0, 0, 0)),
        name="arrange",
    )(*inputs)


def gather(source, filt, shards):
    groups, _, _, rows, lanes = source.shape
    return pl.pallas_call(
        functools.partial(gather_kernel, shards, groups),
        out_shape=(
            jax.ShapeDtypeStruct((shards, groups, 4, rows, lanes), source.dtype),
            jax.ShapeDtypeStruct(filt.shape[:-1] + (lanes,), filt.dtype),
        ),
        in_specs=[WHOLE, ANY],
        out_specs=(ANY, ANY),
        scratch_shapes=[
            pltpu.SemaphoreType.DMA,
            pltpu.SemaphoreType.DMA((groups * 2,)),
            pltpu.SemaphoreType.DMA((groups * 2,)),
            pltpu.SemaphoreType.DMA((groups * shards // 2,)),
            pltpu.SemaphoreType.DMA((groups * shards // 2,)),
            pltpu.SemaphoreType.DMA,
            pltpu.SemaphoreType.DMA,
        ],
        compiler_params=pltpu.CompilerParams(collective_id=0, has_side_effects=True),
        name="gather",
    )(source, filt)


def trade_kernel(shards, source, grad, target, other, own_sem, send_sem, recv_sem):
    s, c = lax.axis_index("seq"), lax.axis_index("chan")
    pairs = shards // 2
    pair, half = s // 2, s % 2
    meet([((pair ^ j) * 2 + half, c) for j in range(1, pairs)] + [(s ^ 1, c)])

    def transfer(j, landing):
        return pltpu.make_async_remote_copy(
            src_ref=source.at[pair ^ j],
            dst_ref=target.at[pair ^ j] if landing else target.at[pair],
            send_sem=send_sem.at[j],
            recv_sem=recv_sem.at[j],
            device_id=((pair ^ j) * 2 + half, c),
            device_id_type=MESH,
        )

    swap = pltpu.make_async_remote_copy(
        src_ref=grad,
        dst_ref=other,
        send_sem=send_sem.at[0],
        recv_sem=recv_sem.at[0],
        device_id=(s ^ 1, c),
        device_id_type=MESH,
    )
    for j in range(pairs - 1, 0, -1):
        transfer(j, False).start()
    swap.start()
    own = pltpu.make_async_copy(source.at[pair], target.at[pair], own_sem)
    own.start()
    own.wait()
    swap.wait_recv()
    for j in range(1, pairs):
        transfer(j, True).wait_recv()
    for j in range(1, pairs):
        transfer(j, False).wait_send()
    swap.wait_send()


def trade(block, grad):
    pairs = block.shape[0]
    return pl.pallas_call(
        functools.partial(trade_kernel, 2 * pairs),
        out_shape=(
            jax.ShapeDtypeStruct(block.shape, block.dtype),
            jax.ShapeDtypeStruct(grad.shape, grad.dtype),
        ),
        in_specs=[WHOLE, ANY],
        out_specs=(ANY, ANY),
        scratch_shapes=[
            pltpu.SemaphoreType.DMA,
            pltpu.SemaphoreType.DMA((pairs,)),
            pltpu.SemaphoreType.DMA((pairs,)),
        ],
        compiler_params=pltpu.CompilerParams(collective_id=1, has_side_effects=True),
        name="trade",
    )(block, grad)


def deliver_kernel(shards, groups, source, target, own_sem, send_sem, recv_sem):
    s, c = lax.axis_index("seq"), lax.axis_index("chan")
    peers = [(j, d) for d in range(groups - 1, -1, -1) for j in range(shards) if j or d]
    meet([(s ^ j, c ^ d) for j, d in peers])

    part, lanes = source.shape[-2:]

    def place(shard, group):
        rows = pl.ds(pl.multiple_of(shard // 2 * part, part), part)
        return target.at[
            :, rows, pl.ds(pl.multiple_of((group * 2 + shard % 2) * lanes, lanes), lanes)
        ]

    def transfer(j, d, landing):
        to_s, to_c = (s ^ j, c ^ d) if landing else (s, c)
        return pltpu.make_async_remote_copy(
            src_ref=source.at[s ^ j, c ^ d],
            dst_ref=place(to_s, to_c),
            send_sem=send_sem.at[d * shards + j],
            recv_sem=recv_sem.at[d * shards + j],
            device_id=(s ^ j, c ^ d),
            device_id_type=MESH,
        )

    for j, d in peers:
        transfer(j, d, False).start()
    own = pltpu.make_async_copy(source.at[s, c], place(s, c), own_sem)
    own.start()
    own.wait()
    for j, d in peers:
        transfer(j, d, True).wait_recv()
    for j, d in peers:
        transfer(j, d, False).wait_send()


def deliver(block):
    shards, groups, _, part, lanes = block.shape
    return pl.pallas_call(
        functools.partial(deliver_kernel, shards, groups),
        out_shape=jax.ShapeDtypeStruct(
            (4, part * shards // 2, groups * 2 * lanes), block.dtype
        ),
        in_specs=[WHOLE],
        out_specs=ANY,
        scratch_shapes=[
            pltpu.SemaphoreType.DMA,
            pltpu.SemaphoreType.DMA((shards * groups,)),
            pltpu.SemaphoreType.DMA((shards * groups,)),
        ],
        compiler_params=pltpu.CompilerParams(collective_id=2, has_side_effects=True),
        name="deliver",
    )(block)


def halves(data):
    high = data.astype(jnp.bfloat16)
    return high, (data - high.astype(jnp.float32)).astype(jnp.bfloat16)


def product(matrix, which, high, low):
    def dot(a, b):
        return jnp.dot(a, b, preferred_element_type=jnp.float32)

    return (
        dot(matrix[which], high) + dot(matrix[which], low) + dot(matrix[which + 1], high)
    )


def spectral_kernel(side, coef, held, turn, matrix, filt, other, grad, away, packed, work):
    shards, groups, _, rows, lanes = held.shape
    length = groups * rows
    total = 2 * length * shards
    part = rows * 2 // shards
    step = pl.program_id(0)
    sign = (1 - 2 * side[0]).astype(jnp.float32)
    turns = jnp.transpose(turn[0])

    def twiddle(w, here):
        return (turns[here, 2 * w : 2 * w + 1], turns[here, 2 * w + 1 : 2 * w + 2])

    for g in range(groups):
        here = pl.ds(g * rows, rows)
        for sig in range(2):
            sums = [[None, None], [None, None]]
            for i in range(shards):
                left = held[i, g, 0 if sig == 0 else 3].astype(jnp.float32)
                right = held[i, g, 1 if sig == 0 else 2].astype(jnp.float32)
                value = left * right
                for p in range(2):
                    term = value * coef[step * 2 + p, i]
                    sums[p][i % 2] = term if i < 2 else sums[p][i % 2] + term
            for w in range(2):
                real, imag = (
                    sums[p][0] + sums[p][1] if w == 0 else sums[p][0] - sums[p][1]
                    for p in range(2)
                )
                cos, sin = twiddle(w, slice(g * rows, (g + 1) * rows))
                at = (w * 2 + sig) * 2 * lanes
                work[here, at : at + lanes] = real * cos + imag * sin
                work[here, at + lanes : at + 2 * lanes] = imag * cos - real * sin
    span = 2 * lanes
    found = []
    for w in range(2):
        spectra = []
        for sig in range(2):
            at = (w * 2 + sig) * span
            high, low = halves(work[:, at : at + span])
            by_cos = product(matrix, 0, high, low)
            by_sin = product(matrix, 2, high, low)
            spectra.append(by_cos[:, :lanes] + by_sin[:, lanes:])
            spectra.append(by_cos[:, lanes:] - by_sin[:, :lanes])
        sr, si, cr, ci = spectra
        spectrum, slope = ((filt, grad), (other, away))[w]
        fr, fi = spectrum[0, 0, 0], spectrum[1, 0, 0]
        slope[0, 0, 0] = (sr * cr + si * ci) * (1.0 / total)
        slope[1, 0, 0] = (sr * ci - si * cr) * (1.0 / total)
        real = (sr * fr - si * fi) - (fr * ci - fi * cr)
        imag = (sr * fi + si * fr) + (fr * cr + fi * ci)
        high, low = halves(jnp.concatenate([real, imag], axis=1))
        by_cos = product(matrix, 0, high, low)
        by_sin = product(matrix, 2, high, low)
        real = by_cos[:, :lanes] - by_sin[:, lanes:]
        imag = by_cos[:, lanes:] + by_sin[:, :lanes]
        cos, sin = (table * (1.0 / total) for table in twiddle(w, slice(None)))
        found.append((real * cos - imag * sin, real * sin + imag * cos))
    for p in range(2):
        done = (found[0][p] + found[1][p], (found[0][p] - found[1][p]) * sign)
        for v in range(2):
            for k in range(shards // 2):
                for g in range(groups):
                    at = g * rows + k * part
                    packed[k, v, 0, p, g * part : (g + 1) * part] = done[v][at : at + part]


def spectral(side, coef, held, turn, matrix, filt, other):
    shards, groups, _, rows, lanes = held.shape
    length = groups * rows
    pairs = shards // 2
    part = length // pairs
    half_block = pl.BlockSpec((2, 1, 1, length, lanes), lambda n, side: (0, 0, n, 0, 0))
    return pl.pallas_call(
        spectral_kernel,
        grid_spec=pltpu.PrefetchScalarGridSpec(
            num_scalar_prefetch=1,
            grid=(2,),
            in_specs=[
                pl.BlockSpec(memory_space=pltpu.SMEM),
                pl.BlockSpec((shards, groups, 4, rows, lanes), lambda n, side: (0, 0, 0, 0, 0)),
                pl.BlockSpec((1, 8, length), lambda n, side: (n, 0, 0)),
                pl.BlockSpec((4, length, length), lambda n, side: (0, 0, 0)),
                pl.BlockSpec((2, 1, 1, length, lanes), lambda n, side: (0, 0, n, 0, side[0])),
                half_block,
            ],
            out_specs=(
                half_block,
                half_block,
                pl.BlockSpec((pairs, 2, 1, 2, part, lanes), lambda n, side: (0, 0, n, 0, 0, 0)),
            ),
            scratch_shapes=[pltpu.VMEM((length, 8 * lanes), jnp.float32)],
        ),
        out_shape=(
            jax.ShapeDtypeStruct(other.shape, jnp.float32),
            jax.ShapeDtypeStruct(other.shape, jnp.float32),
            jax.ShapeDtypeStruct((pairs, 2, 2, 2, part, lanes), jnp.float32),
        ),
        compiler_params=pltpu.CompilerParams(vmem_limit_bytes=60 * 1024 * 1024),
        name="spectral",
    )(side, coef, held, turn, matrix, filt, other)


def rotate(value, numerator, denominator):
    numerator = numerator % denominator
    real, imag = value
    if numerator == 0:
        return value
    if 4 * numerator == denominator:
        return (-imag, real)
    angle = 2.0 * math.pi * numerator / denominator
    cos, sin = math.cos(angle), math.sin(angle)
    return (real * cos - imag * sin, real * sin + imag * cos)


def butterflies(values):
    count = len(values)
    if count == 1:
        return values
    even, odd = butterflies(values[0::2]), butterflies(values[1::2])
    out = [None] * count
    for k in range(count // 2):
        turned = rotate(odd[k], k, count)
        out[k] = (even[k][0] + turned[0], even[k][1] + turned[1])
        out[k + count // 2] = (even[k][0] - turned[0], even[k][1] - turned[1])
    return out


def finish_kernel(pair, pieces, gates, result):
    shards, _, _, part, lanes = gates.shape
    pairs = shards // 2
    bits = pairs.bit_length() - 1
    ladders = {}
    for e in range(2):
        for v in range(2):
            terms = []
            for q in range(pairs):
                k = mirrored(q, bits)
                terms.append(rotate((pieces[k, v, e, 0], pieces[k, v, e, 1]), q * v, shards))
            ladders[e, v] = butterflies(terms)
    for i in range(shards):
        plain = ladders[0, i % 2][i // 2]
        odd = rotate(ladders[1, i % 2][i // 2], i, 2 * shards)
        conv = plain[0] + odd[0]
        back = plain[1] + odd[1]
        value = gates[i, 0, 0].astype(jnp.float32)
        gate_in = gates[i, 0, 1].astype(jnp.float32)
        gate_out = gates[i, 0, 2].astype(jnp.float32)
        incoming = gates[i, 0, 3].astype(jnp.float32)
        result[i, 0, 0] = (gate_out * conv).astype(jnp.bfloat16)
        result[i, 0, 1] = (back * gate_in).astype(jnp.bfloat16)
        result[i, 0, 2] = (back * value).astype(jnp.bfloat16)
        result[i, 0, 3] = (incoming * conv).astype(jnp.bfloat16)


def finish(pair, pieces, held):
    shards, groups, _, rows, lanes = held.shape
    part = rows * 2 // shards
    block = (shards, 1, 4, part, lanes)
    return pl.pallas_call(
        finish_kernel,
        grid_spec=pltpu.PrefetchScalarGridSpec(
            num_scalar_prefetch=1,
            grid=(groups,),
            in_specs=[
                pl.BlockSpec((shards // 2, 2, 2, 2, part, lanes), lambda n, k: (0, 0, 0, 0, n, 0)),
                pl.BlockSpec(block, lambda n, k: (0, n, 0, k[0], 0)),
            ],
            out_specs=pl.BlockSpec(block, lambda n, k: (0, n, 0, 0, 0)),
        ),
        out_shape=jax.ShapeDtypeStruct((shards, groups, 4, part, lanes), jnp.bfloat16),
        name="finish",
    )(pair[None], pieces, held)


def transform_matrix(length):
    counter = np.arange(length)
    angle = 2.0 * math.pi * (np.outer(counter, counter) % length) / length
    out = []
    for table in (np.cos(angle), np.sin(angle)):
        high = table.astype(jnp.bfloat16)
        out += [high, (table - high.astype(np.float64)).astype(jnp.bfloat16)]
    return jnp.asarray(np.stack(out))


def on_device(shards, groups, values_in, gate_in, gate_out, cotangent, filter_spectra):
    rows = values_in.shape[0]
    length = rows * groups
    total = 2 * length * shards
    index = lax.axis_index("seq")
    side = index % 2
    own = 2 * mirrored(index, shards.bit_length() - 1) + jnp.arange(2, dtype=jnp.int32)
    shard = jnp.arange(shards, dtype=jnp.int32)
    angle = (2.0 * math.pi / (2 * shards)) * (own[:, None] * shard[None, :] % (2 * shards)).astype(
        jnp.float32
    )
    coef = jnp.stack([jnp.cos(angle), -jnp.sin(angle)], axis=1).reshape(4, shards)
    position = jnp.arange(length, dtype=jnp.int32)
    residue = jnp.stack([own, (own + shards) % (2 * shards)], axis=1)
    angle = (2.0 * math.pi / total) * (residue[..., None] * position % total).astype(jnp.float32)
    turn = jnp.stack([jnp.cos(angle), jnp.sin(angle)], axis=2).reshape(2, 4, length)
    turn = jnp.concatenate([turn, jnp.zeros_like(turn)], axis=1)

    source = arrange((values_in, gate_in, gate_out, cotangent), groups)
    held, other = gather(source, filter_spectra, shards)
    mine, away, packed = spectral(
        side[None], coef, held, turn, transform_matrix(length), filter_spectra, other
    )
    pieces, theirs = trade(packed, away)
    outs = deliver(finish(index // 2, pieces, held))
    grad_filter = jnp.concatenate(
        [jnp.where(side == 0, mine, theirs), jnp.where(side == 0, theirs, mine)], axis=-1
    )
    return (outs[0], outs[1], outs[2], outs[3], grad_filter)


def solution(mesh):
    tokens = P(("seq", "chan"), None)
    spectrum = P(None, "seq", None, None, "chan")
    return jax.shard_map(
        functools.partial(on_device, mesh.shape["seq"], mesh.shape["chan"]),
        mesh=mesh,
        in_specs=(tokens, tokens, tokens, tokens, spectrum),
        out_specs=(tokens, tokens, tokens, tokens, spectrum),
        check_vma=False,
    )
```

profile of v0, /device:TPU:0, one launch (start us, length us, event | category | flops | bytes accessed | tf_op | source)
XLA Modules:
  0.0 140.0 jit_solution(6539419699690482591)
XLA Ops:
  0.7 0.1 pad_add_fusion
  0.8 0.1 fusion.9
  0.9 0.6 pad_maximum_fusion.2
  1.5 0.3 fusion.4
  1.9 0.6 concatenate.6.turn
  2.5 3.4 %arrange.1.refs_0_ = bf16[4,2,4,128,128]{4,3,2,1,0:T(8,128)(2,1)} custom-call(bf16[128,1024]{1,0:T(8,128)(2,1)} %refs_0_.1, bf16[128,1024]{1,0:T(8,128)(2,1)} %refs_1_.2, bf16[128,1024]{1,0:T(8,128)(2,1)} %refs_2_.1, bf16[128,1024]{1,0:T(8,128)(2,1)} %refs_3_.1), custom_call_target="tpu_custom_call" | custom-call | tf_op jit(solution)/shard_map/arrange/pallas_call | solution.py:125
  5.9 52.7 %gather.1 = (bf16[8,4,4,128,128]{4,3,2,1,0:T(8,128)(2,1)}, f32[2,1,2,512,128]{4,3,2,1,0:T(8,128)}) custom-call(bf16[4,2,4,128,128]{4,3,2,1,0:T(8,128)(2,1)} %arrange.1.refs_0_, f32[2,1,2,512,256]{4,3,2,1,0:T(8,128)} %filt.1), custom_call_target="tpu_custom_call" | custom-call | tf_op jit(solution)/shard_map/gather/pallas_call | solution.py:137
  58.6 17.0 %spectral.1 = (f32[2,1,2,512,128]{4,3,2,1,0:T(8,128)}, f32[2,1,2,512,128]{4,3,2,1,0:T(8,128)}, f32[4,2,2,2,128,128]{5,4,3,2,1,0:T(8,128)}) custom-call(s32[1]{0:T(128)} %bitcast.1.side, f32[4,8]{1,0:T(4,128)} %bitcast.11, bf16[8,4,4,128,128]{4,3,2,1,0:T(8,128)(2,1)} %get-tuple-element.12.held.gates, f32[2,8,512]{2,1,0:T(8,128)} %concatenate.6.turn, ...), custom_call_target="tpu_custom_call" | custom-call | tf_op jit(solution)/shard_map/spectral/pallas_call | solution.py:357
  75.6 26.7 %trade.1 = (f32[4,2,2,2,128,128]{5,4,3,2,1,0:T(8,128)}, f32[2,1,2,512,128]{4,3,2,1,0:T(8,128)}) custom-call(f32[4,2,2,2,128,128]{5,4,3,2,1,0:T(8,128)} %get-tuple-element.14.source, f32[2,1,2,512,128]{4,3,2,1,0:T(8,128)} %get-tuple-element.15.grad), custom_call_target="tpu_custom_call" | custom-call | tf_op jit(solution)/shard_map/trade/pallas_call | solution.py:199
  102.3 4.0 %finish.1.source = bf16[8,4,4,32,128]{4,3,2,1,0:T(8,128)(2,1)} custom-call(s32[1]{0:T(128)} %bitcast.pair, f32[4,2,2,2,128,128]{5,4,3,2,1,0:T(8,128)} %get-tuple-element.16.pieces, bf16[8,4,4,128,128]{4,3,2,1,0:T(8,128)(2,1)} %get-tuple-element.12.held.gates), custom_call_target="tpu_custom_call" | custom-call | tf_op jit(solution)/shard_map/finish/pallas_call | solution.py:443
  106.2 0.0 copy-start
  106.3 0.0 copy-start.1
  106.3 29.9 %deliver.1 = bf16[4,128,1024]{2,1,0:T(8,128)(2,1)} custom-call(bf16[8,4,4,32,128]{4,3,2,1,0:T(8,128)(2,1)} %finish.1.source), custom_call_target="tpu_custom_call" | custom-call | tf_op jit(solution)/shard_map/deliver/pallas_call | solution.py:254
  136.2 2.2 %slice_bitcast_fusion = (bf16[128,1024]{1,0:T(8,128)(2,1)}, bf16[128,1024]{1,0:T(8,128)(2,1)}, bf16[128,1024]{1,0:T(8,128)(2,1)}, bf16[128,1024]{1,0:T(8,128)(2,1)}) fusion(bf16[4,128,1024]{2,1,0:T(8,128)(2,1)} %deliver.1), kind=kLoop, calls=%fused_computation.3 | loop fusion | bytes 2097152 | tf_op jit(solution)/shard_map/squeeze | solution.py:497
  138.4 0.0 copy-done
  138.4 0.0 copy-done.1
  138.4 0.1 broadcast_select_fusion.1
  138.5 1.5 %pad_maximum_fusion = f32[2,1,2,512,256]{4,3,2,1,0:T(8,128)} fusion(f32[2,1,2,512,128]{4,3,2,1,0:T(8,128)S(1)} %get-tuple-element.20, f32[2,1,2,512,128]{4,3,2,1,0:T(8,128)S(1)} %get-tuple-element.19), kind=kLoop, calls=%fused_computation | loop fusion | flops 524288 | bytes 4194304 | tf_op jit(solution)/shard_map/concatenate | solution.py:494
  (4 shorter events, 0.1 us)
Async XLA Ops:
  106.2 32.1 %copy-start = (f32[2,1,2,512,128]{4,3,2,1,0:T(8,128)S(1)}, f32[2,1,2,512,128]{4,3,2,1,0:T(8,128)}, u32[]{:S(2)}) copy-start(f32[2,1,2,512,128]{4,3,2,1,0:T(8,128)} %get-tuple-element.17) | copy-start | bytes 3145732
  106.3 32.1 %copy-start.1 = (f32[2,1,2,512,128]{4,3,2,1,0:T(8,128)S(1)}, f32[2,1,2,512,128]{4,3,2,1,0:T(8,128)}, u32[]{:S(2)}) copy-start(f32[2,1,2,512,128]{4,3,2,1,0:T(8,128)} %get-tuple-element.18) | copy-start | bytes 3145732
where the time goes:
time: 140 us
  Pallas kernels  134 us (96%)
  local copies, waits for them, and re-layouts  2.82 us (2%)
  other arithmetic  2.76 us (2%)
    pallas_call x1, Pallas kernels, gather(): pl.pallas_call(functools.partial(gather_kernel, shards, groups), out_shap...  52.7 us
    pallas_call x1, Pallas kernels, deliver(): pl.pallas_call(functools.partial(deliver_kernel, shards, groups), out_sha...  29.9 us
    pallas_call x1, Pallas kernels, trade(): pl.pallas_call(functools.partial(trade_kernel, 2 * pairs), out_shape=(jax...  26.7 us
    pallas_call x1, Pallas kernels, spectral(): pl.pallas_call(spectral_kernel, grid_spec=pltpu.PrefetchScalarGridSpec(nu...  17 us
    pallas_call x1, Pallas kernels, finish(): pl.pallas_call(finish_kernel, grid_spec=pltpu.PrefetchScalarGridSpec(num_...  3.98 us
    pallas_call x1, Pallas kernels, arrange(): pl.pallas_call(arrange_kernel, grid=(groups,), out_shape=jax.ShapeDtypeSt...  3.4 us

commit v1 on v0

v1 whole, which is shorter than its diff:
```python
import functools
import math

import jax
import jax.numpy as jnp
import numpy as np
from jax import lax
from jax.experimental import pallas as pl
from jax.experimental.pallas import tpu as pltpu
from jax.sharding import PartitionSpec as P

MESH = pl.DeviceIdType.MESH
ANY = pl.BlockSpec(memory_space=pl.ANY)
WHOLE = pl.BlockSpec(memory_space=pltpu.VMEM)
LANES = 128
STEPS = 4


def mirrored(number, bits):
    out = 0
    for place in range(bits):
        out = out + ((number >> place) & 1) * (1 << (bits - 1 - place))
    return out


def meet(peers):
    barrier = pltpu.get_barrier_semaphore()
    for peer in peers:
        pl.semaphore_signal(barrier, inc=1, device_id=peer, device_id_type=MESH)
    pl.semaphore_wait(barrier, len(peers))


def lane_group(width):
    return lax.broadcasted_iota(jnp.int32, (1, LANES), 1) // width


def swap_lanes(arrays, width):
    arrays = list(arrays)
    group = lane_group(width)
    bit = 1
    while bit < len(arrays):
        low = (group & bit) == 0
        shift = bit * width
        for i in range(len(arrays)):
            if i & bit:
                continue
            a, b = arrays[i], arrays[i | bit]
            arrays[i] = jnp.where(low, a, pltpu.roll(b, shift, 1))
            arrays[i | bit] = jnp.where(low, pltpu.roll(a, LANES - shift, 1), b)
        bit *= 2
    return arrays


def halves(data):
    high = data.astype(jnp.bfloat16)
    return high, (data - high.astype(jnp.float32)).astype(jnp.bfloat16)


def add(a, b):
    if a is None:
        return b
    return a if b is None else a + b


def sub(a, b):
    if b is None:
        return a
    return -b if a is None else a - b


def scale(a, factor):
    if a is None or abs(factor) < 1e-12:
        return None
    if abs(factor - 1.0) < 1e-12:
        return a
    return -a if abs(factor + 1.0) < 1e-12 else a * factor


def turned(value, numerator, denominator):
    angle = 2.0 * math.pi * numerator / denominator
    cos, sin = math.cos(angle), math.sin(angle)
    real, imag = value
    return (
        sub(scale(real, cos), scale(imag, sin)),
        add(scale(real, sin), scale(imag, cos)),
    )


def conjugate(value):
    return (value[0], scale(value[1], -1.0))


def forward_ladder(values):
    if len(values) == 1:
        return [(values[0], None), (values[0], None)]
    count = 2 * len(values)
    even, odd = forward_ladder(values[0::2]), forward_ladder(values[1::2])
    out = [None] * (count // 2 + 1)
    for k in range(count // 4 + 1):
        spun = turned(odd[k], -k, count)
        out[k] = (add(even[k][0], spun[0]), add(even[k][1], spun[1]))
        if k != count // 4:
            away = (sub(even[k][0], spun[0]), sub(even[k][1], spun[1]))
            out[count // 2 - k] = conjugate(away)
    return out


def inverse_ladder(values):
    if len(values) == 2:
        return [add(values[0][0], values[1][0])]
    half = len(values) - 1
    even, odd = [], []
    for k in range(half // 2):
        a, b = values[k], conjugate(values[half - k])
        even.append((add(a[0], b[0]), add(a[1], b[1])))
        odd.append(turned((sub(a[0], b[0]), sub(a[1], b[1])), k, 2 * half))
    even.append(values[half // 2])
    odd.append(turned(values[half // 2], 1, 4))
    out = [None] * half
    out[0::2], out[1::2] = inverse_ladder(even), inverse_ladder(odd)
    return out


def arrange_kernel(width, *refs):
    inputs, filt, source, hsrc, hspec = refs[:4], *refs[4:]
    fan, rows = source.shape[0], source.shape[2]
    for a in range(4):
        block = inputs[a][...].astype(jnp.float32)
        parts = [block[g * rows : (g + 1) * rows] for g in range(fan)]
        for u, part in enumerate(swap_lanes(parts, width)):
            source[u, a] = part.astype(jnp.bfloat16)
    pack = fan // 4
    span = filt.shape[3] // 2
    even = [
        filt[p, e, q, pl.ds(0, span, stride=2), :]
        for q in range(pack)
        for p in range(2)
        for e in range(2)
    ]
    for u, part in enumerate(swap_lanes(even, width)):
        hsrc[u] = part
    odd = [
        filt[p, 0, q, pl.ds(1 + half * span, span // 2, stride=2), :]
        for q in range(pack)
        for half in range(2)
        for p in range(2)
    ]
    for u, part in enumerate(swap_lanes(odd, width)):
        hspec[u] = part


def arrange(inputs, filt, devices, shards):
    rows, channels = inputs[0].shape
    width = channels // devices
    fan = LANES // width
    pack = fan // 4
    length = filt.shape[3]
    blocks = channels // LANES
    part = blocks // STEPS
    wide = length // pack
    return pl.pallas_call(
        functools.partial(arrange_kernel, width),
        grid=(blocks,),
        out_shape=(
            jax.ShapeDtypeStruct((devices, 4, rows // fan, LANES), jnp.bfloat16),
            jax.ShapeDtypeStruct((shards, wide // 2, LANES), jnp.float32),
            jax.ShapeDtypeStruct((shards, wide // 4, LANES), jnp.float32),
        ),
        in_specs=[pl.BlockSpec((rows, LANES), lambda t: (0, t))] * 4
        + [
            pl.BlockSpec(
                (2, 2, pack, wide // STEPS, LANES),
                lambda t: (0, 0, 0, t % STEPS, t // STEPS),
            )
        ],
        out_specs=(
            pl.BlockSpec((fan, 4, rows // fan, LANES), lambda t: (t, 0, 0, 0)),
            pl.BlockSpec((fan, wide // 2 // STEPS, LANES), lambda t: (t // STEPS, t % STEPS, 0)),
            pl.BlockSpec((fan, wide // 4 // STEPS, LANES), lambda t: (t // STEPS, t % STEPS, 0)),
        ),
        name="arrange",
    )(*inputs, filt.reshape(2, 2, pack, wide, filt.shape[4]))


def scatter_kernel(source, hsrc, hspec, held, hheld, special, *sems):
    own_sem, t_send, t_recv, f_send, f_recv, x_send, x_recv = sems
    groups, shards = source.shape[:2]
    s, c = lax.axis_index("seq"), lax.axis_index("chan")
    peers = [(j, d) for d in range(groups - 1, -1, -1) for j in range(shards) if j or d]
    meet([(s ^ j, c ^ d) for j, d in peers])

    def tokens(j, d, landing):
        to_s, to_c = (s ^ j, c ^ d) if landing else (s, c)
        return pltpu.make_async_remote_copy(
            src_ref=source.at[c ^ d, s ^ j],
            dst_ref=held.at[to_s, to_c],
            send_sem=t_send.at[d * shards + j],
            recv_sem=t_recv.at[d * shards + j],
            device_id=(s ^ j, c ^ d),
            device_id_type=MESH,
        )

    def spectrum(j, landing):
        return pltpu.make_async_remote_copy(
            src_ref=hsrc.at[s ^ j],
            dst_ref=hheld.at[s ^ j] if landing else hheld.at[s],
            send_sem=f_send.at[j],
            recv_sem=f_recv.at[j],
            device_id=(s ^ j, c),
            device_id_type=MESH,
        )

    def extra(j):
        return pltpu.make_async_remote_copy(
            src_ref=hspec.at[j],
            dst_ref=special,
            send_sem=x_send.at[j],
            recv_sem=x_recv,
            device_id=(j, c),
            device_id_type=MESH,
        )

    for j, d in peers:
        tokens(j, d, False).start()
    for j in range(1, shards):
        spectrum(j, False).start()

    @pl.when(s == 0)
    def _():
        for j in range(1, shards):
            extra(j).start()

    locals_ = [
        pltpu.make_async_copy(source.at[c, s], held.at[s, c], own_sem.at[0]),
        pltpu.make_async_copy(hsrc.at[s], hheld.at[s], own_sem.at[1]),
    ]
    for copy in locals_:
        copy.start()

    @pl.when(s == 0)
    def _():
        copy = pltpu.make_async_copy(hspec.at[0], special, own_sem.at[2])
        copy.start()
        copy.wait()
        for j in range(1, shards):
            extra(j).wait_send()

    @pl.when(s != 0)
    def _():
        extra(s).wait_recv()

    for copy in locals_:
        copy.wait()
    for j, d in peers:
        tokens(j, d, True).wait_recv()
    for j in range(1, shards):
        spectrum(j, True).wait_recv()
    for j, d in peers:
        tokens(j, d, False).wait_send()
    for j in range(1, shards):
        spectrum(j, False).wait_send()


def scatter(source, hsrc, hspec):
    groups, shards = source.shape[:2]
    dma = pltpu.SemaphoreType.DMA
    return pl.pallas_call(
        scatter_kernel,
        out_shape=(
            jax.ShapeDtypeStruct((shards, groups) + source.shape[2:], source.dtype),
            jax.ShapeDtypeStruct(hsrc.shape, hsrc.dtype),
            jax.ShapeDtypeStruct(hspec.shape[1:], hspec.dtype),
        ),
        in_specs=[WHOLE] * 3,
        out_specs=(ANY, ANY, ANY),
        scratch_shapes=[
            dma((3,)),
            dma((groups * shards,)),
            dma((groups * shards,)),
            dma((shards,)),
            dma((shards,)),
            dma((shards,)),
            dma,
        ],
        compiler_params=pltpu.CompilerParams(collective_id=0, has_side_effects=True),
        name="scatter",
    )(source, hsrc, hspec)


def residues(shards, fan):
    bits = shards.bit_length() - 1
    flat = [2 * mirrored(r, bits) + e for r in range(shards) for e in range(2)]
    sets = [flat[i : i + fan] for i in range(0, len(flat), fan)]
    return sets + [[2 * shards] + [None] * (fan - 1)]


def transform(matrix, high, low):
    def dot(a, b):
        return jnp.dot(a, b, preferred_element_type=jnp.float32)

    return dot(matrix[0], high) + dot(matrix[0], low) + dot(matrix[1], high)


def spectral_kernel(
    fan, held, hheld, special, matrix, twiddle, result, grads, y_high, y_low, v_work, flipped
):
    shards, groups, _, rows, _ = held.shape
    bits = shards.bit_length() - 1
    length = matrix.shape[1] // 2
    sets = residues(shards, fan)
    width = LANES // fan
    pack = fan // 4
    main = len(sets) - 1
    total = 4 * shards * length
    spread = rows * fan
    near = groups // 2
    step = min(rows, 16)
    chunks = rows // step

    def zero():
        return jnp.zeros((step, LANES), jnp.float32)

    def forward(k, carry):
        c1, piece = k // chunks, k % chunks
        here = pl.ds(pl.multiple_of(piece * step, step), step)
        for sig in range(2):
            values = []
            for b in range(2 * shards):
                block = held.at[b // 2, (b % 2) * near + c1]
                left = block[0 if sig == 0 else 3, here].astype(jnp.float32)
                right = block[1 if sig == 0 else 2, here].astype(jnp.float32)
                values.append(left * right)
            found = forward_ladder(values)
            for n, slots in enumerate(sets):
                sides = []
                for p in range(2):
                    arrays = [None if f is None else found[f][p] for f in slots]
                    sides.append(
                        swap_lanes([zero() if a is None else a for a in arrays], width)
                    )
                for g in range(fan):
                    at = pl.multiple_of(c1 * spread + g * rows + piece * step, step)
                    spot = pl.ds(at, step)
                    cos, sin = twiddle[n, 0, spot, :], twiddle[n, 1, spot, :]
                    real, imag = sides[0][g], sides[1][g]
                    high, low = halves(real * cos + imag * sin)
                    lanes = slice(sig * LANES, (sig + 1) * LANES)
                    y_high[n, spot, lanes] = high
                    y_low[n, spot, lanes] = low
                    high, low = halves(imag * cos - real * sin)
                    spot = pl.ds(pl.multiple_of(length + at, step), step)
                    y_high[n, spot, lanes] = high
                    y_low[n, spot, lanes] = low
        return carry

    lax.fori_loop(0, near * chunks, forward, 0)

    flip = (
        lax.broadcasted_iota(jnp.int32, (length, length), 0)
        + lax.broadcasted_iota(jnp.int32, (length, length), 1)
        == length - 1
    )
    flip = jnp.where(flip, 1.0, 0.0).astype(jnp.bfloat16)
    share = length // pack
    first = lane_group(width) == 0
    even_lane = (lane_group(width) & 1) == 0
    extra = None

    def packets(real, imag):
        arrays = []
        for q in range(pack):
            arrays += [real[q * share : (q + 1) * share], imag[q * share : (q + 1) * share]]
        return swap_lanes(arrays, 2 * width)

    for n in range(main + 1):
        spectra = transform(matrix, y_high[n], y_low[n])
        sr, cr = spectra[:length, :LANES], spectra[:length, LANES:]
        si, ci = spectra[length:, :LANES], spectra[length:, LANES:]
        if n < main:
            devices = [n * (fan // 2) + i for i in range(fan // 2)]
            found = swap_lanes([hheld[r] for r in devices], 2 * width)
            fr = jnp.concatenate(found[0::2], axis=0)
            fi = jnp.concatenate(found[1::2], axis=0)
        else:
            small = length // 4 // 2 // pack
            pieces = [[], []]
            for q in range(pack):
                for t in range(STEPS):
                    for half in range(2):
                        block = special[t * small : (t + 1) * small]
                        for p in range(2):
                            shift = ((q * 2 + half) * 2 + p) * width
                            moved = pltpu.roll(block, LANES - shift, 1) if shift else block
                            pieces[p].append(jnp.where(first, moved, 0.0))
            fr, fi = (jnp.concatenate(piece, axis=0) for piece in pieces)
        slope_real = (sr * cr + si * ci) * (1.0 / total)
        slope_imag = (sr * ci - si * cr) * (1.0 / total)
        if n < main:
            for r, part in zip(devices, packets(slope_real, slope_imag)):
                grads[r, pl.ds(0, share, stride=2), :] = part
            slopes = jnp.concatenate([slope_real, slope_imag], axis=1)
            high, low = halves(slopes)
            turned_over = jnp.dot(flip, high, preferred_element_type=jnp.float32) + jnp.dot(
                flip, low, preferred_element_type=jnp.float32
            )
            for r, part in zip(devices, packets(turned_over[:, :LANES], -turned_over[:, LANES:])):
                flipped[r] = part
        else:
            extra = jnp.zeros((share, LANES), jnp.float32)
            for q in range(pack):
                for p, slope in enumerate((slope_real, slope_imag)):
                    place = (q * 2 + p) * 2
                    moved = slope[q * share : (q + 1) * share]
                    moved = pltpu.roll(moved, place * width, 1) if place else moved
                    extra = jnp.where(lane_group(width) == place, moved, extra)
        weight = jnp.full((1, LANES), 2.0 / total, jnp.float32)
        if None in sets[n] or 0 in sets[n]:
            weight = jnp.where(first, 1.0 / total, weight)
        conv = ((sr * fr - si * fi) * weight, (sr * fi + si * fr) * weight)
        back = ((cr * fr + ci * fi) * weight, (ci * fr - cr * fi) * weight)
        stacked = jnp.concatenate(
            [
                jnp.concatenate([conv[0], back[0]], axis=1),
                jnp.concatenate([-conv[1], -back[1]], axis=1),
            ],
            axis=0,
        )
        high, low = halves(stacked)
        found = transform(matrix, high, low)
        cos = jnp.concatenate([twiddle[n, 0]] * 2, axis=1)
        sin = jnp.concatenate([twiddle[n, 1]] * 2, axis=1)
        real, against = found[:length], found[length:]
        v_work[n, 0] = real * cos + against * sin
        v_work[n, 1] = real * sin - against * cos

    for r in range(shards):
        place = mirrored(r, bits)
        near_even = flipped[mirrored(shards - place, bits)] if place else extra
        near_odd = flipped[shards - 1 - r]
        grads[r, pl.ds(1, share, stride=2), :] = jnp.where(even_lane, near_even, near_odd)

    def inverse(k, carry):
        c1, piece = k // chunks, k % chunks
        here = pl.ds(pl.multiple_of(piece * step, step), step)
        for sig in range(2):
            values = [[None, None] for _ in range(2 * shards + 1)]
            for n, slots in enumerate(sets):
                for p in range(2):
                    arrays = []
                    for g in range(fan):
                        at = pl.multiple_of(c1 * spread + g * rows + piece * step, step)
                        lanes = slice(sig * LANES, (sig + 1) * LANES)
                        arrays.append(v_work[n, p, pl.ds(at, step), lanes])
                    for f, array in zip(slots, swap_lanes(arrays, width)):
                        if f is not None:
                            values[f][p] = array
            for b, value in enumerate(inverse_ladder([tuple(v) for v in values])):
                result[b // 2, (b % 2) * near + c1, sig, here, :] = value
        return carry

    lax.fori_loop(0, near * chunks, inverse, 0)


def spectral(held, hheld, special, tables, fan):
    shards, groups, _, rows, _ = held.shape
    matrix, twiddle = tables
    sets, _, length, _ = twiddle.shape
    return pl.pallas_call(
        functools.partial(spectral_kernel, fan),
        out_shape=(
            jax.ShapeDtypeStruct((shards, groups, 2, rows, LANES), jnp.float32),
            jax.ShapeDtypeStruct((shards, 2 * hheld.shape[1], LANES), jnp.float32),
        ),
        in_specs=[WHOLE] * 5,
        out_specs=(WHOLE, WHOLE),
        scratch_shapes=[
            pltpu.VMEM((sets, 2 * length, 2 * LANES), jnp.bfloat16),
            pltpu.VMEM((sets, 2 * length, 2 * LANES), jnp.bfloat16),
            pltpu.VMEM((sets, 2, length, 2 * LANES), jnp.float32),
            pltpu.VMEM(hheld.shape, jnp.float32),
        ],
        compiler_params=pltpu.CompilerParams(vmem_limit_bytes=48 * 1024 * 1024),
        name="spectral",
    )(held, hheld, special, matrix, twiddle)


def deliver_kernel(source, grads, target, landed, own_sem, t_send, t_recv, g_send, g_recv):
    shards, groups = source.shape[:2]
    s, c = lax.axis_index("seq"), lax.axis_index("chan")
    peers = [(j, d) for d in range(groups - 1, -1, -1) for j in range(shards) if j or d]
    meet([(s ^ j, c ^ d) for j, d in peers])

    def tokens(j, d, landing):
        to_s, to_c = (s ^ j, c ^ d) if landing else (s, c)
        return pltpu.make_async_remote_copy(
            src_ref=source.at[s ^ j, c ^ d],
            dst_ref=target.at[to_c, to_s],
            send_sem=t_send.at[d * shards + j],
            recv_sem=t_recv.at[d * shards + j],
            device_id=(s ^ j, c ^ d),
            device_id_type=MESH,
        )

    def slopes(j, landing):
        return pltpu.make_async_remote_copy(
            src_ref=grads.at[s ^ j],
            dst_ref=landed.at[s ^ j] if landing else landed.at[s],
            send_sem=g_send.at[j],
            recv_sem=g_recv.at[j],
            device_id=(s ^ j, c),
            device_id_type=MESH,
        )

    for j in range(1, shards):
        slopes(j, False).start()
    for j, d in peers:
        tokens(j, d, False).start()
    locals_ = [
        pltpu.make_async_copy(source.at[s, c], target.at[c, s], own_sem.at[0]),
        pltpu.make_async_copy(grads.at[s], landed.at[s], own_sem.at[1]),
    ]
    for copy in locals_:
        copy.start()
    for copy in locals_:
        copy.wait()
    for j, d in peers:
        tokens(j, d, True).wait_recv()
    for j in range(1, shards):
        slopes(j, True).wait_recv()
    for j, d in peers:
        tokens(j, d, False).wait_send()
    for j in range(1, shards):
        slopes(j, False).wait_send()


def deliver(source, grads):
    shards, groups = source.shape[:2]
    dma = pltpu.SemaphoreType.DMA
    return pl.pallas_call(
        deliver_kernel,
        out_shape=(
            jax.ShapeDtypeStruct((groups, shards) + source.shape[2:], source.dtype),
            jax.ShapeDtypeStruct(grads.shape, grads.dtype),
        ),
        in_specs=[WHOLE] * 2,
        out_specs=(ANY, ANY),
        scratch_shapes=[
            dma((2,)),
            dma((groups * shards,)),
            dma((groups * shards,)),
            dma((shards,)),
            dma((shards,)),
        ],
        compiler_params=pltpu.CompilerParams(collective_id=1, has_side_effects=True),
        name="deliver",
    )(source, grads)


def finish_kernel(width, values, gate_in, gate_out, cotangent, found, landed, *outs):
    fan, rows = found.shape[0], found.shape[2]
    conv = swap_lanes([found[u, 0] for u in range(fan)], width)
    back = swap_lanes([found[u, 1] for u in range(fan)], width)
    for g in range(fan):
        here = slice(g * rows, (g + 1) * rows)

        def wide(ref):
            return ref[here].astype(jnp.float32)

        outs[0][here] = (wide(gate_out) * conv[g]).astype(jnp.bfloat16)
        outs[1][here] = (back[g] * wide(gate_in)).astype(jnp.bfloat16)
        outs[2][here] = (back[g] * wide(values)).astype(jnp.bfloat16)
        outs[3][here] = (wide(cotangent) * conv[g]).astype(jnp.bfloat16)
    slopes = swap_lanes([landed[u] for u in range(fan)], width)
    for i, slope in enumerate(slopes):
        outs[4][i // 2 % 2, i % 2, i // 4] = slope


def finish(inputs, found, landed, filt):
    rows, channels = inputs[0].shape
    devices, _, short, _ = found.shape
    width = channels // devices
    fan = LANES // width
    pack = fan // 4
    wide = landed.shape[1]
    column = pl.BlockSpec((rows, LANES), lambda t: (0, t))
    blocks = channels // LANES
    outs = pl.pallas_call(
        functools.partial(finish_kernel, width),
        grid=(blocks,),
        out_shape=tuple(jax.ShapeDtypeStruct((rows, channels), jnp.bfloat16) for _ in range(4))
        + (jax.ShapeDtypeStruct((2, 2, pack, wide, filt.shape[4]), jnp.float32),),
        in_specs=[column] * 4
        + [
            pl.BlockSpec((fan, 2, short, LANES), lambda t: (t, 0, 0, 0)),
            pl.BlockSpec((fan, wide // STEPS, LANES), lambda t: (t // STEPS, t % STEPS, 0)),
        ],
        out_specs=(column,) * 4
        + (
            pl.BlockSpec(
                (2, 2, pack, wide // STEPS, LANES),
                lambda t: (0, 0, 0, t % STEPS, t // STEPS),
            ),
        ),
        name="finish",
    )(*inputs, found, landed)
    return outs[:4] + (outs[4].reshape(filt.shape),)


def make_tables(shards, fan, length):
    counter = np.arange(length)
    angle = 2.0 * math.pi * (np.outer(counter, counter) % length) / length
    cos, sin = np.cos(angle), np.sin(angle)
    whole = np.block([[cos, sin], [-sin, cos]])
    high = whole.astype(jnp.bfloat16)
    low = (whole - high.astype(np.float64)).astype(jnp.bfloat16)
    total = 4 * shards * length
    turns = []
    for slots in residues(shards, fan):
        lanes = np.repeat([0 if f is None else f for f in slots], LANES // fan)
        turn = 2.0 * math.pi * (counter[:, None] * lanes[None, :] % total) / total
        turns.append(np.stack([np.cos(turn), np.sin(turn)]))
    twiddle = np.stack(turns).astype(np.float32)
    return jnp.asarray(np.stack([high, low])), jnp.asarray(twiddle)


def on_device(shards, groups, values_in, gate_in, gate_out, cotangent, filter_spectra):
    inputs = (values_in, gate_in, gate_out, cotangent)
    rows, channels = values_in.shape
    devices = shards * groups
    fan = LANES * devices // channels
    source, hsrc, hspec = arrange(inputs, filter_spectra, devices, shards)
    source = source.reshape((groups, shards) + source.shape[1:])
    held, hheld, special = scatter(source, hsrc, hspec)
    tables = make_tables(shards, fan, rows * groups // 2)
    result, grads = spectral(held, hheld, special, tables, fan)
    found, landed = deliver(result, grads)
    found = found.reshape((devices,) + found.shape[2:])
    return finish(inputs, found, landed, filter_spectra)


def solution(mesh):
    tokens = P(("seq", "chan"), None)
    spectrum = P(None, "seq", None, None, "chan")
    return jax.shard_map(
        functools.partial(on_device, mesh.shape["seq"], mesh.shape["chan"]),
        mesh=mesh,
        in_specs=(tokens, tokens, tokens, tokens, spectrum),
        out_specs=(tokens, tokens, tokens, tokens, spectrum),
        check_vma=False,
    )
```

time: 140 us -> 111 us (0.79)
  Pallas kernels: 134 us -> 106 us
  other arithmetic: 2.76 us -> 0 us
  local copies, waits for them, and re-layouts: 2.82 us -> 4.28 us
    pallas_call x6 -> x5, Pallas kernels: 134 us -> 106 us  [the longest x1 41.4 us: deliver(): pl.pallas_call(deliver_kernel, out_shape=(jax.ShapeDtypeStruct((groups, s...]
    unnamed x4 -> x12, local copies, waits for them, and re-layouts: 0.01 us -> 4.28 us
    squeeze x1 -> x0, local copies, waits for them, and re-layouts: 2.17 us -> none  [on_device(): return (outs[0], outs[1], outs[2], outs[3], grad_filter)]
    concatenate x1 -> x0, other arithmetic: 1.46 us -> none  [on_device(): jnp.concatenate([jnp.where(side == 0, mine, theirs), jnp.where(side == 0,...]
where the time goes in v1:
time: 111 us
  Pallas kernels  106 us (95%)
  local copies, waits for them, and re-layouts  4.28 us (4%)
    pallas_call x1, Pallas kernels, deliver(): pl.pallas_call(deliver_kernel, out_shape=(jax.ShapeDtypeStruct((groups, s...  41.4 us
    pallas_call x1, Pallas kernels, scatter(): pl.pallas_call(scatter_kernel, out_shape=(jax.ShapeDtypeStruct((shards, g...  36 us
    pallas_call x1, Pallas kernels, spectral(): pl.pallas_call(functools.partial(spectral_kernel, fan), out_shape=(jax.Sh...  13.9 us
    pallas_call x1, Pallas kernels, finish(): pl.pallas_call(functools.partial(finish_kernel, width), grid=(blocks,), o...  7.49 us
    pallas_call x1, Pallas kernels, arrange(): pl.pallas_call(functools.partial(arrange_kernel, width), grid=(blocks,),...  7.08 us
    unnamed x12, local copies, waits for them, and re-layouts  4.28 us

profile of v1, /device:TPU:0, one launch (start us, length us, event | category | flops | bytes accessed | tf_op | source)
XLA Modules:
  0.0 110.8 jit_solution(4466202267288935977)
XLA Ops:
  0.6 7.1 %arrange.1 = (bf16[32,4,32,128]{3,2,1,0:T(8,128)(2,1)}, f32[8,256,128]{2,1,0:T(8,128)}, f32[8,128,128]{2,1,0:T(8,128)}) custom-call(bf16[128,1024]{1,0:T(8,128)(2,1)} %values.1, bf16[128,1024]{1,0:T(8,128)(2,1)} %gate_in.1, bf16[128,1024]{1,0:T(8,128)(2,1)} %gate_out.1, bf16[128,1024]{1,0:T(8,128)(2,1)} %cotangent.1, f32[2,2,1,512,256]{4,3,2,1,0:T(8,128)} %bitcast.6), custom_call_target="tpu_custom_call" | custom-call | tf_op jit(solution)/shard_map/arrange/pallas_call | solution.py:161
  7.7 0.0 copy-start
  7.7 0.0 copy-start.1
  7.7 36.0 %scatter.1 = (bf16[8,4,4,32,128]{4,3,2,1,0:T(8,128)(2,1)}, f32[8,256,128]{2,1,0:T(8,128)}, f32[128,128]{1,0:T(8,128)}) custom-call(bf16[4,8,4,32,128]{4,3,2,1,0:T(8,128)(2,1)} %bitcast.7, f32[8,256,128]{2,1,0:T(8,128)} %get-tuple-element.21.hsrc, f32[8,128,128]{2,1,0:T(8,128)} %get-tuple-element.22.hspec), custom_call_target="tpu_custom_call" | custom-call | tf_op jit(solution)/shard_map/scatter/pallas_call | solution.py:267
  43.7 0.0 copy-done
  43.7 0.0 copy-done.1
  43.7 0.0 copy-start.2
  43.7 1.2 %copy-done.2 = bf16[8,4,4,32,128]{4,3,2,1,0:T(8,128)(2,1)S(1)} copy-done((bf16[8,4,4,32,128]{4,3,2,1,0:T(8,128)(2,1)S(1)}, bf16[8,4,4,32,128]{4,3,2,1,0:T(8,128)(2,1)}, u32[]{:S(2)}) %copy-start.2) | copy-done | bytes 1048600
  44.9 0.0 copy-start.3
  44.9 1.2 %copy-done.3 = f32[8,256,128]{2,1,0:T(8,128)S(1)} copy-done((f32[8,256,128]{2,1,0:T(8,128)S(1)}, f32[8,256,128]{2,1,0:T(8,128)}, u32[]{:S(2)}) %copy-start.3) | copy-done | bytes 1048600
  46.2 0.0 copy-start.5
  46.2 0.8 copy-done.5
  47.0 13.9 %spectral.1 = (f32[8,4,2,32,128]{4,3,2,1,0:T(8,128)S(1)}, f32[8,512,128]{2,1,0:T(8,128)}) custom-call(bf16[8,4,4,32,128]{4,3,2,1,0:T(8,128)(2,1)S(1)} %copy-done.2, f32[8,256,128]{2,1,0:T(8,128)S(1)} %copy-done.3, f32[128,128]{1,0:T(8,128)S(1)} %copy-done.5, bf16[2,512,512]{2,1,0:T(8,128)(2,1)S(1)} %copy-done.1, f32[5,2,256,128]{3,2,1,0:T(8,128)S(1)} %copy-done), custom_call_target="tpu_custom_call" | custom-call | tf_op jit(solution)/shard_map/spectral/pallas_call | solution.py:468
  60.9 0.0 copy-start.4
  60.9 1.0 copy-done.4
  61.9 41.4 %deliver.1 = (f32[4,8,2,32,128]{4,3,2,1,0:T(8,128)}, f32[8,512,128]{2,1,0:T(8,128)}) custom-call(f32[8,4,2,32,128]{4,3,2,1,0:T(8,128)} %copy-done.4, f32[8,512,128]{2,1,0:T(8,128)} %get-tuple-element.27.grads), custom_call_target="tpu_custom_call" | custom-call | tf_op jit(solution)/shard_map/deliver/pallas_call | solution.py:539
  103.3 7.5 %finish.1 = (bf16[128,1024]{1,0:T(8,128)(2,1)}, bf16[128,1024]{1,0:T(8,128)(2,1)}, bf16[128,1024]{1,0:T(8,128)(2,1)}, bf16[128,1024]{1,0:T(8,128)(2,1)}, f32[2,2,1,512,256]{4,3,2,1,0:T(8,128)}) custom-call(bf16[128,1024]{1,0:T(8,128)(2,1)} %values.1, bf16[128,1024]{1,0:T(8,128)(2,1)} %gate_in.1, bf16[128,1024]{1,0:T(8,128)(2,1)} %gate_out.1, ...), custom_call_target="tpu_custom_call" | custom-call | tf_op jit(solution)/shard_map/finish/pallas_call | solution.py:587
Async XLA Ops:
  7.7 36.0 %copy-start = (f32[5,2,256,128]{3,2,1,0:T(8,128)S(1)}, f32[5,2,256,128]{3,2,1,0:T(8,128)}, u32[]{:S(2)}) copy-start(f32[5,2,256,128]{3,2,1,0:T(8,128)} %constant.5.clone.twiddle) | copy-start | bytes 3932164
  7.7 36.0 %copy-start.1 = (bf16[2,512,512]{2,1,0:T(8,128)(2,1)S(1)}, bf16[2,512,512]{2,1,0:T(8,128)(2,1)}, u32[]{:S(2)}) copy-start(bf16[2,512,512]{2,1,0:T(8,128)(2,1)} %constant.4.clone.matrix) | copy-start | bytes 3145732
  43.7 1.2 %copy-start.2 = (bf16[8,4,4,32,128]{4,3,2,1,0:T(8,128)(2,1)S(1)}, bf16[8,4,4,32,128]{4,3,2,1,0:T(8,128)(2,1)}, u32[]{:S(2)}) copy-start(bf16[8,4,4,32,128]{4,3,2,1,0:T(8,128)(2,1)} %get-tuple-element.23.held) | copy-start | bytes 3145732
  44.9 1.2 %copy-start.3 = (f32[8,256,128]{2,1,0:T(8,128)S(1)}, f32[8,256,128]{2,1,0:T(8,128)}, u32[]{:S(2)}) copy-start(f32[8,256,128]{2,1,0:T(8,128)} %get-tuple-element.24.hheld) | copy-start | bytes 3145732
  46.2 0.8 copy-start.5
  60.9 1.0 copy-start.4

commit v2 on v1

v2 whole, which is shorter than its diff:
```python
import functools
import math

import jax
import jax.numpy as jnp
import numpy as np
from jax import lax
from jax.experimental import pallas as pl
from jax.experimental.pallas import tpu as pltpu
from jax.sharding import PartitionSpec as P

MESH = pl.DeviceIdType.MESH
ANY = pl.BlockSpec(memory_space=pl.ANY)
LANES = 128
STEPS = 4


def mirrored(number, bits):
    out = 0
    for place in range(bits):
        out = out + ((number >> place) & 1) * (1 << (bits - 1 - place))
    return out


def lane_group(width):
    return lax.broadcasted_iota(jnp.int32, (1, LANES), 1) // width


def swap_lanes(arrays, width):
    arrays = list(arrays)
    group = lane_group(width)
    bit = 1
    while bit < len(arrays):
        low = (group & bit) == 0
        shift = bit * width
        for i in range(len(arrays)):
            if i & bit:
                continue
            a, b = arrays[i], arrays[i | bit]
            arrays[i] = jnp.where(low, a, pltpu.roll(b, shift, 1))
            arrays[i | bit] = jnp.where(low, pltpu.roll(a, LANES - shift, 1), b)
        bit *= 2
    return arrays


def halves(data):
    high = data.astype(jnp.bfloat16)
    return high, (data - high.astype(jnp.float32)).astype(jnp.bfloat16)


def add(a, b):
    if a is None:
        return b
    return a if b is None else a + b


def sub(a, b):
    if b is None:
        return a
    return -b if a is None else a - b


def scale(a, factor):
    if a is None or abs(factor) < 1e-12:
        return None
    if abs(factor - 1.0) < 1e-12:
        return a
    return -a if abs(factor + 1.0) < 1e-12 else a * factor


def turned(value, numerator, denominator):
    angle = 2.0 * math.pi * numerator / denominator
    cos, sin = math.cos(angle), math.sin(angle)
    real, imag = value
    return (
        sub(scale(real, cos), scale(imag, sin)),
        add(scale(real, sin), scale(imag, cos)),
    )


def conjugate(value):
    return (value[0], scale(value[1], -1.0))


def forward_ladder(values):
    if len(values) == 1:
        return [(values[0], None), (values[0], None)]
    count = 2 * len(values)
    even, odd = forward_ladder(values[0::2]), forward_ladder(values[1::2])
    out = [None] * (count // 2 + 1)
    for k in range(count // 4 + 1):
        spun = turned(odd[k], -k, count)
        out[k] = (add(even[k][0], spun[0]), add(even[k][1], spun[1]))
        if k != count // 4:
            away = (sub(even[k][0], spun[0]), sub(even[k][1], spun[1]))
            out[count // 2 - k] = conjugate(away)
    return out


def inverse_ladder(values):
    if len(values) == 2:
        return [add(values[0][0], values[1][0])]
    half = len(values) - 1
    even, odd = [], []
    for k in range(half // 2):
        a, b = values[k], conjugate(values[half - k])
        even.append((add(a[0], b[0]), add(a[1], b[1])))
        odd.append(turned((sub(a[0], b[0]), sub(a[1], b[1])), k, 2 * half))
    even.append(values[half // 2])
    odd.append(turned(values[half // 2], 1, 4))
    out = [None] * half
    out[0::2], out[1::2] = inverse_ladder(even), inverse_ladder(odd)
    return out


def residues(shards, fan):
    bits = shards.bit_length() - 1
    flat = [2 * mirrored(r, bits) + e for r in range(shards) for e in range(2)]
    sets = [flat[i : i + fan] for i in range(0, len(flat), fan)]
    return sets + [[2 * shards] + [None] * (fan - 1)]


def transform(matrix, high, low):
    def dot(a, b):
        return jnp.dot(a, b, preferred_element_type=jnp.float32)

    return dot(matrix[0], high) + dot(matrix[0], low) + dot(matrix[1], high)


def convolve_kernel(shards, groups, *refs):
    inputs, filt, matrix_in, twiddle_in, found, landed = refs[:4], *refs[4:9]
    (
        tokens,
        raw,
        matrix,
        twiddle,
        source,
        hsrc,
        hspec,
        held,
        hheld,
        special,
        y_high,
        y_low,
        v_work,
        flipped,
        grads,
        result,
        in_sem,
        own_sem,
        t_send,
        t_recv,
        f_send,
        f_recv,
        x_send,
        x_recv,
        g_send,
        g_recv,
        r_send,
        r_recv,
    ) = refs[9:]
    s, c = lax.axis_index("seq"), lax.axis_index("chan")
    devices = shards * groups
    rows = source.shape[2]
    channels = tokens.shape[2]
    width = channels // devices
    fan = LANES // width
    pack = fan // 4
    blocks = channels // LANES
    near = groups // 2
    bits = shards.bit_length() - 1
    length = matrix.shape[1] // 2
    total = 4 * shards * length
    spread = rows * fan
    step = min(rows, 16)
    chunks = rows // step
    share = length // pack
    sets = residues(shards, fan)
    main = len(sets) - 1

    loads = [pltpu.make_async_copy(inputs[a], tokens.at[a], in_sem.at[a]) for a in range(4)]
    loads.append(pltpu.make_async_copy(matrix_in, matrix, in_sem.at[4]))
    loads.append(pltpu.make_async_copy(twiddle_in, twiddle, in_sem.at[5]))
    for i in range(raw.shape[0]):
        part = filt.at[:, :, :, :, pl.ds(i * LANES, LANES)]
        loads.append(pltpu.make_async_copy(part, raw.at[i], in_sem.at[6 + i]))
    for load in loads:
        load.start()

    peers = [(j, d) for d in range(groups - 1, -1, -1) for j in range(shards) if j or d]
    barrier = pltpu.get_barrier_semaphore()
    for j, d in peers:
        pl.semaphore_signal(barrier, inc=1, device_id=(s ^ j, c ^ d), device_id_type=MESH)

    def token(j, d, landing):
        to_s, to_c = (s ^ j, c ^ d) if landing else (s, c)
        return pltpu.make_async_remote_copy(
            src_ref=source.at[(c ^ d) * shards + (s ^ j)],
            dst_ref=held.at[to_s, to_c],
            send_sem=t_send.at[d * shards + j],
            recv_sem=t_recv.at[d * shards + j],
            device_id=(s ^ j, c ^ d),
            device_id_type=MESH,
        )

    def spectrum(j, landing):
        return pltpu.make_async_remote_copy(
            src_ref=hsrc.at[s ^ j],
            dst_ref=hheld.at[s ^ j] if landing else hheld.at[s],
            send_sem=f_send.at[j],
            recv_sem=f_recv.at[j],
            device_id=(s ^ j, c),
            device_id_type=MESH,
        )

    def extra(j):
        return pltpu.make_async_remote_copy(
            src_ref=hspec.at[j],
            dst_ref=special,
            send_sem=x_send.at[j],
            recv_sem=x_recv,
            device_id=(j, c),
            device_id_type=MESH,
        )

    def slope(odd, r):
        return pltpu.make_async_remote_copy(
            src_ref=grads.at[odd, r],
            dst_ref=landed.at[odd, s],
            send_sem=g_send.at[odd, r],
            recv_sem=g_recv.at[odd, s],
            device_id=(r, c),
            device_id_type=MESH,
        )

    def arrival(odd, r):
        return pltpu.make_async_remote_copy(
            src_ref=grads.at[odd, r],
            dst_ref=landed.at[odd, r],
            send_sem=g_send.at[odd, r],
            recv_sem=g_recv.at[odd, r],
            device_id=(r, c),
            device_id_type=MESH,
        )

    def outcome(j, d, landing):
        to_s, to_c = (s ^ j, c ^ d) if landing else (s, c)
        return pltpu.make_async_remote_copy(
            src_ref=result.at[s ^ j, c ^ d],
            dst_ref=found.at[to_c * shards + to_s],
            send_sem=r_send.at[d * shards + j],
            recv_sem=r_recv.at[d * shards + j],
            device_id=(s ^ j, c ^ d),
            device_id_type=MESH,
        )

    for a in range(4):
        loads[a].wait()

    def arrange(t, carry):
        lanes = pl.ds(pl.multiple_of(t * LANES, LANES), LANES)
        for a in range(4):
            parts = [
                tokens[a, g * rows : (g + 1) * rows, lanes].astype(jnp.float32)
                for g in range(fan)
            ]
            for u, part in enumerate(swap_lanes(parts, width)):
                source[t * fan + u, a] = part.astype(jnp.bfloat16)
        return carry

    lax.fori_loop(0, blocks, arrange, 0)
    pl.semaphore_wait(barrier, len(peers))
    for j, d in peers:
        token(j, d, False).start()

    for load in loads[6:]:
        load.wait()
    wide = raw.shape[4]
    span = wide // 2 // STEPS

    def arrange_filter(t, carry):
        column, piece = t // STEPS, t % STEPS
        base = pl.multiple_of(piece * 2 * span, 2 * span)
        even = [
            raw[column, p, e, q, pl.ds(base, span, stride=2), :]
            for q in range(pack)
            for p in range(2)
            for e in range(2)
        ]
        for u, part in enumerate(swap_lanes(even, width)):
            hsrc[column * fan + u, pl.ds(pl.multiple_of(piece * span, span), span)] = part
        odd = [
            raw[column, p, 0, q, pl.ds(base + 1 + half * span, span // 2, stride=2), :]
            for q in range(pack)
            for half in range(2)
            for p in range(2)
        ]
        half_span = span // 2
        for u, part in enumerate(swap_lanes(odd, width)):
            at = pl.ds(pl.multiple_of(piece * half_span, half_span), half_span)
            hspec[column * fan + u, at] = part
        return carry

    lax.fori_loop(0, raw.shape[0] * STEPS, arrange_filter, 0)
    for j in range(1, shards):
        spectrum(j, False).start()
    own = [
        pltpu.make_async_copy(source.at[c * shards + s], held.at[s, c], own_sem.at[0]),
        pltpu.make_async_copy(hsrc.at[s], hheld.at[s], own_sem.at[1]),
    ]
    for copy in own:
        copy.start()

    @pl.when(s == 0)
    def _():
        for j in range(1, shards):
            extra(j).start()
        copy = pltpu.make_async_copy(hspec.at[0], special, own_sem.at[2])
        copy.start()
        copy.wait()

    own[0].wait()
    for j, d in peers:
        token(j, d, True).wait_recv()
    loads[4].wait()
    loads[5].wait()

    def zero():
        return jnp.zeros((step, LANES), jnp.float32)

    def forward(k, carry):
        c1, piece = k // chunks, k % chunks
        here = pl.ds(pl.multiple_of(piece * step, step), step)
        for sig in range(2):
            values = []
            for b in range(2 * shards):
                block = held.at[b // 2, (b % 2) * near + c1]
                left = block[0 if sig == 0 else 3, here].astype(jnp.float32)
                right = block[1 if sig == 0 else 2, here].astype(jnp.float32)
                values.append(left * right)
            ladder = forward_ladder(values)
            for n, slots in enumerate(sets):
                sides = []
                for p in range(2):
                    arrays = [None if f is None else ladder[f][p] for f in slots]
                    sides.append(
                        swap_lanes([zero() if a is None else a for a in arrays], width)
                    )
                for g in range(fan):
                    at = pl.multiple_of(c1 * spread + g * rows + piece * step, step)
                    spot = pl.ds(at, step)
                    cos, sin = twiddle[n, 0, spot, :], twiddle[n, 1, spot, :]
                    real, imag = sides[0][g], sides[1][g]
                    high, low = halves(real * cos + imag * sin)
                    lanes = slice(sig * LANES, (sig + 1) * LANES)
                    y_high[n, spot, lanes] = high
                    y_low[n, spot, lanes] = low
                    high, low = halves(imag * cos - real * sin)
                    spot = pl.ds(pl.multiple_of(length + at, step), step)
                    y_high[n, spot, lanes] = high
                    y_low[n, spot, lanes] = low
        return carry

    lax.fori_loop(0, near * chunks, forward, 0)

    flip = (
        lax.broadcasted_iota(jnp.int32, (length, length), 0)
        + lax.broadcasted_iota(jnp.int32, (length, length), 1)
        == length - 1
    )
    flip = jnp.where(flip, 1.0, 0.0).astype(jnp.bfloat16)
    first = lane_group(width) == 0
    even_lane = (lane_group(width) & 1) == 0

    def packets(real, imag):
        arrays = []
        for q in range(pack):
            arrays += [real[q * share : (q + 1) * share], imag[q * share : (q + 1) * share]]
        return swap_lanes(arrays, 2 * width)

    def members(n):
        return [n * (fan // 2) + i for i in range(fan // 2)] if n < main else []

    def send(odd, r):
        @pl.when(s != r)
        def _():
            slope(odd, r).start()

    for n in range(main + 1):
        spectra = transform(matrix, y_high[n], y_low[n])
        v_work[n, 0], v_work[n, 1] = spectra[:length], spectra[length:]
        sr, cr = spectra[:length, :LANES], spectra[:length, LANES:]
        si, ci = spectra[length:, :LANES], spectra[length:, LANES:]
        slope_real = (sr * cr + si * ci) * (1.0 / total)
        slope_imag = (sr * ci - si * cr) * (1.0 / total)
        if n < main:
            for r, part in zip(members(n), packets(slope_real, slope_imag)):
                grads[0, r] = part
            high, low = halves(jnp.concatenate([slope_real, slope_imag], axis=1))
            turned_over = jnp.dot(flip, high, preferred_element_type=jnp.float32) + jnp.dot(
                flip, low, preferred_element_type=jnp.float32
            )
            for r, part in zip(
                members(n), packets(turned_over[:, :LANES], -turned_over[:, LANES:])
            ):
                flipped[r] = part
        else:
            last = jnp.zeros((share, LANES), jnp.float32)
            for q in range(pack):
                for p, side in enumerate((slope_real, slope_imag)):
                    place = (q * 2 + p) * 2
                    moved = side[q * share : (q + 1) * share]
                    moved = pltpu.roll(moved, place * width, 1) if place else moved
                    last = jnp.where(lane_group(width) == place, moved, last)
        if n:
            for r in members(n - 1):
                send(0, r)

    for r in range(shards):
        place = mirrored(r, bits)
        near_even = flipped[mirrored(shards - place, bits)] if place else last
        grads[1, r] = jnp.where(even_lane, near_even, flipped[shards - 1 - r])

    own[1].wait()
    for j in range(1, shards):
        spectrum(j, True).wait_recv()

    @pl.when(s != 0)
    def _():
        extra(s).wait_recv()

    for n in range(main + 1):
        if n < main:
            filters = swap_lanes([hheld[r] for r in members(n)], 2 * width)
            fr = jnp.concatenate(filters[0::2], axis=0)
            fi = jnp.concatenate(filters[1::2], axis=0)
        else:
            small = length // 4 // 2 // pack
            pieces = [[], []]
            for q in range(pack):
                for t in range(STEPS):
                    for half in range(2):
                        block = special[t * small : (t + 1) * small]
                        for p in range(2):
                            shift = ((q * 2 + half) * 2 + p) * width
                            moved = pltpu.roll(block, LANES - shift, 1) if shift else block
                            pieces[p].append(jnp.where(first, moved, 0.0))
            fr, fi = (jnp.concatenate(piece, axis=0) for piece in pieces)
        weight = jnp.full((1, LANES), 2.0 / total, jnp.float32)
        if None in sets[n] or 0 in sets[n]:
            weight = jnp.where(first, 1.0 / total, weight)
        fr, fi = fr * weight, fi * weight
        sr, cr = v_work[n, 0, :, :LANES], v_work[n, 0, :, LANES:]
        si, ci = v_work[n, 1, :, :LANES], v_work[n, 1, :, LANES:]
        stacked = jnp.concatenate(
            [
                jnp.concatenate([sr * fr - si * fi, cr * fr + ci * fi], axis=1),
                jnp.concatenate([-(sr * fi + si * fr), cr * fi - ci * fr], axis=1),
            ],
            axis=0,
        )
        high, low = halves(stacked)
        sums = transform(matrix, high, low)
        cos = jnp.concatenate([twiddle[n, 0]] * 2, axis=1)
        sin = jnp.concatenate([twiddle[n, 1]] * 2, axis=1)
        real, against = sums[:length], sums[length:]
        v_work[n, 0] = real * cos + against * sin
        v_work[n, 1] = real * sin - against * cos
        if n == 0:
            for r in range(shards):
                send(1, r)

    mine = [
        pltpu.make_async_copy(grads.at[odd, s], landed.at[odd, s], own_sem.at[3 + odd])
        for odd in range(2)
    ]
    for copy in mine:
        copy.start()

    def inverse(k, carry):
        c1, piece = k // chunks, k % chunks
        here = pl.ds(pl.multiple_of(piece * step, step), step)
        for sig in range(2):
            values = [[None, None] for _ in range(2 * shards + 1)]
            for n, slots in enumerate(sets):
                for p in range(2):
                    arrays = []
                    for g in range(fan):
                        at = pl.multiple_of(c1 * spread + g * rows + piece * step, step)
                        lanes = slice(sig * LANES, (sig + 1) * LANES)
                        arrays.append(v_work[n, p, pl.ds(at, step), lanes])
                    for f, array in zip(slots, swap_lanes(arrays, width)):
                        if f is not None:
                            values[f][p] = array
            for b, value in enumerate(inverse_ladder([tuple(v) for v in values])):
                result[b // 2, (b % 2) * near + c1, sig, here, :] = value
        return carry

    lax.fori_loop(0, near * chunks, inverse, 0)
    for j, d in peers:
        outcome(j, d, False).start()
    rest = pltpu.make_async_copy(result.at[s, c], found.at[c * shards + s], own_sem.at[5])
    rest.start()

    for j, d in peers:
        token(j, d, False).wait_send()
    for j in range(1, shards):
        spectrum(j, False).wait_send()

    @pl.when(s == 0)
    def _():
        for j in range(1, shards):
            extra(j).wait_send()

    for copy in mine + [rest]:
        copy.wait()
    for odd in range(2):
        for r in range(shards):

            @pl.when(s != r)
            def _():
                arrival(odd, r).wait_recv()
                slope(odd, r).wait_send()

    for j, d in peers:
        outcome(j, d, True).wait_recv()
    for j, d in peers:
        outcome(j, d, False).wait_send()


def convolve(inputs, filt, tables, shards, groups):
    rows, channels = inputs[0].shape
    devices = shards * groups
    width = channels // devices
    fan = LANES // width
    pack = fan // 4
    short = rows // fan
    matrix, twiddle = tables
    sets, _, length, _ = twiddle.shape
    share = length // pack
    raw = filt.reshape(2, 2, pack, 2 * share, filt.shape[4])
    dma, vmem = pltpu.SemaphoreType.DMA, pltpu.VMEM
    f32, bf16 = jnp.float32, jnp.bfloat16
    return pl.pallas_call(
        functools.partial(convolve_kernel, shards, groups),
        out_shape=(
            jax.ShapeDtypeStruct((devices, 2, short, LANES), f32),
            jax.ShapeDtypeStruct((2, shards, share, LANES), f32),
        ),
        in_specs=[ANY] * 7,
        out_specs=(ANY, ANY),
        scratch_shapes=[
            vmem((4, rows, channels), bf16),
            vmem((raw.shape[4] // LANES,) + raw.shape[:4] + (LANES,), f32),
            vmem(matrix.shape, bf16),
            vmem(twiddle.shape, f32),
            vmem((devices, 4, short, LANES), bf16),
            vmem((shards, share, LANES), f32),
            vmem((shards, share // 2, LANES), f32),
            vmem((shards, groups, 4, short, LANES), bf16),
            vmem((shards, share, LANES), f32),
            vmem((share // 2, LANES), f32),
            vmem((sets, 2 * length, 2 * LANES), bf16),
            vmem((sets, 2 * length, 2 * LANES), bf16),
            vmem((sets, 2, length, 2 * LANES), f32),
            vmem((shards, share, LANES), f32),
            vmem((2, shards, share, LANES), f32),
            vmem((shards, groups, 2, short, LANES), f32),
            dma((6 + raw.shape[4] // LANES,)),
            dma((6,)),
            dma((devices,)),
            dma((devices,)),
            dma((shards,)),
            dma((shards,)),
            dma((shards,)),
            dma,
            dma((2, shards)),
            dma((2, shards)),
            dma((devices,)),
            dma((devices,)),
        ],
        compiler_params=pltpu.CompilerParams(
            collective_id=0, has_side_effects=True, vmem_limit_bytes=48 * 1024 * 1024
        ),
        name="convolve",
    )(*inputs, raw, matrix, twiddle)


def finish_kernel(width, values, gate_in, gate_out, cotangent, found, landed, *outs):
    rows = found.shape[2]
    fan = landed.shape[1]
    for block in range(found.shape[0] // fan):
        parts = [found.at[block * fan + u] for u in range(fan)]
        conv = swap_lanes([part[0] for part in parts], width)
        back = swap_lanes([part[1] for part in parts], width)
        lanes = slice(block * LANES, (block + 1) * LANES)
        for g in range(fan):
            here = slice(g * rows, (g + 1) * rows)

            def wide(ref):
                return ref[here, lanes].astype(jnp.float32)

            outs[0][here, lanes] = (wide(gate_out) * conv[g]).astype(jnp.bfloat16)
            outs[1][here, lanes] = (back[g] * wide(gate_in)).astype(jnp.bfloat16)
            outs[2][here, lanes] = (back[g] * wide(values)).astype(jnp.bfloat16)
            outs[3][here, lanes] = (wide(cotangent) * conv[g]).astype(jnp.bfloat16)
    span = landed.shape[2]
    for odd in range(2):
        for i, slope in enumerate(swap_lanes([landed[odd, u] for u in range(fan)], width)):
            outs[4][i // 2 % 2, i % 2, i // 4, pl.ds(odd, span, stride=2), :] = slope


def finish(inputs, found, landed, filt):
    rows, channels = inputs[0].shape
    devices, _, short, _ = found.shape
    width = channels // devices
    fan = LANES // width
    pack = fan // 4
    share = landed.shape[2]
    tiles = channels // LANES // STEPS
    column = pl.BlockSpec((rows, tiles * LANES), lambda t: (0, t))
    pieces = STEPS * LANES // filt.shape[4]
    outs = pl.pallas_call(
        functools.partial(finish_kernel, width),
        grid=(STEPS,),
        out_shape=tuple(jax.ShapeDtypeStruct((rows, channels), jnp.bfloat16) for _ in range(4))
        + (jax.ShapeDtypeStruct((2, 2, pack, 2 * share, filt.shape[4]), jnp.float32),),
        in_specs=[column] * 4
        + [
            pl.BlockSpec((tiles * fan, 2, short, LANES), lambda t: (t, 0, 0, 0)),
            pl.BlockSpec(
                (2, fan, share // pieces, LANES), lambda t: (0, t // pieces, t % pieces, 0)
            ),
        ],
        out_specs=(column,) * 4
        + (
            pl.BlockSpec(
                (2, 2, pack, 2 * share // pieces, LANES),
                lambda t: (0, 0, 0, t % pieces, t // pieces),
            ),
        ),
        name="finish",
    )(*inputs, found, landed)
    return outs[:4] + (outs[4].reshape(filt.shape),)


def make_tables(shards, fan, length):
    counter = np.arange(length)
    angle = 2.0 * math.pi * (np.outer(counter, counter) % length) / length
    cos, sin = np.cos(angle), np.sin(angle)
    whole = np.block([[cos, sin], [-sin, cos]])
    high = whole.astype(jnp.bfloat16)
    low = (whole - high.astype(np.float64)).astype(jnp.bfloat16)
    total = 4 * shards * length
    turns = []
    for slots in residues(shards, fan):
        lanes = np.repeat([0 if f is None else f for f in slots], LANES // fan)
        turn = 2.0 * math.pi * (counter[:, None] * lanes[None, :] % total) / total
        turns.append(np.stack([np.cos(turn), np.sin(turn)]))
    twiddle = np.stack(turns).astype(np.float32)
    return jnp.asarray(np.stack([high, low])), jnp.asarray(twiddle)


def on_device(shards, groups, values_in, gate_in, gate_out, cotangent, filter_spectra):
    inputs = (values_in, gate_in, gate_out, cotangent)
    rows, channels = values_in.shape
    fan = LANES * shards * groups // channels
    tables = make_tables(shards, fan, rows * groups // 2)
    found, landed = convolve(inputs, filter_spectra, tables, shards, groups)
    return finish(inputs, found, landed, filter_spectra)


def solution(mesh):
    tokens = P(("seq", "chan"), None)
    spectrum = P(None, "seq", None, None, "chan")
    return jax.shard_map(
        functools.partial(on_device, mesh.shape["seq"], mesh.shape["chan"]),
        mesh=mesh,
        in_specs=(tokens, tokens, tokens, tokens, spectrum),
        out_specs=(tokens, tokens, tokens, tokens, spectrum),
        check_vma=False,
    )
```

time: 111 us -> 90.6 us (0.82)
  Pallas kernels: 106 us -> 82.2 us
  local copies, waits for them, and re-layouts: 4.28 us -> 7.31 us
    pallas_call x5 -> x2, Pallas kernels: 106 us -> 82.2 us  [the longest x1 76.5 us: convolve(): pl.pallas_call(functools.partial(convolve_kernel, shards, groups), out_sh...]
    unnamed x12 -> x14, local copies, waits for them, and re-layouts: 4.28 us -> 7.31 us
where the time goes in v2:
time: 90.6 us; the launch traced here: 90.2 us
  Pallas kernels  82.2 us (91%)
  local copies, waits for them, and re-layouts  7.31 us (8%)
    pallas_call x1, Pallas kernels, convolve(): pl.pallas_call(functools.partial(convolve_kernel, shards, groups), out_sh...  76.5 us
    unnamed x14, local copies, waits for them, and re-layouts  7.31 us
    pallas_call x1, Pallas kernels, finish(): pl.pallas_call(functools.partial(finish_kernel, width), grid=(STEPS,), ou...  5.75 us

profile of v2, /device:TPU:0, one launch (start us, length us, event | category | flops | bytes accessed | tf_op | source)
XLA Modules:
  0.0 90.2 jit_solution(9280999158569316811)
XLA Ops:
  0.6 0.0 copy-start
  0.6 1.3 %copy-done = f32[5,2,256,128]{3,2,1,0:T(8,128)S(1)} copy-done((f32[5,2,256,128]{3,2,1,0:T(8,128)S(1)}, f32[5,2,256,128]{3,2,1,0:T(8,128)}, u32[]{:S(2)}) %copy-start) | copy-done | bytes 1310744
  2.0 0.0 copy-start.2
  2.0 1.2 %copy-done.2 = bf16[2,512,512]{2,1,0:T(8,128)(2,1)S(1)} copy-done((bf16[2,512,512]{2,1,0:T(8,128)(2,1)S(1)}, bf16[2,512,512]{2,1,0:T(8,128)(2,1)}, u32[]{:S(2)}) %copy-start.2) | copy-done | bytes 1048600
  3.2 0.0 copy-start.3
  3.2 0.9 %copy-done.3 = bf16[128,1024]{1,0:T(8,128)(2,1)S(1)} copy-done((bf16[128,1024]{1,0:T(8,128)(2,1)S(1)}, bf16[128,1024]{1,0:T(8,128)(2,1)}, u32[]{:S(2)}) %copy-start.3) | copy-done | bytes 262168
  4.1 0.0 copy-start.4
  4.1 0.9 %copy-done.4 = bf16[128,1024]{1,0:T(8,128)(2,1)S(1)} copy-done((bf16[128,1024]{1,0:T(8,128)(2,1)S(1)}, bf16[128,1024]{1,0:T(8,128)(2,1)}, u32[]{:S(2)}) %copy-start.4) | copy-done | bytes 262168
  5.1 0.0 copy-start.5
  5.1 0.9 %copy-done.5 = bf16[128,1024]{1,0:T(8,128)(2,1)S(1)} copy-done((bf16[128,1024]{1,0:T(8,128)(2,1)S(1)}, bf16[128,1024]{1,0:T(8,128)(2,1)}, u32[]{:S(2)}) %copy-start.5) | copy-done | bytes 262168
  6.0 0.0 copy-start.6
  6.0 0.9 %copy-done.6 = bf16[128,1024]{1,0:T(8,128)(2,1)S(1)} copy-done((bf16[128,1024]{1,0:T(8,128)(2,1)S(1)}, bf16[128,1024]{1,0:T(8,128)(2,1)}, u32[]{:S(2)}) %copy-start.6) | copy-done | bytes 262168
  7.0 76.5 %convolve.1 = (f32[32,2,32,128]{3,2,1,0:T(8,128)S(1)}, f32[2,8,256,128]{3,2,1,0:T(8,128)}) custom-call(bf16[128,1024]{1,0:T(8,128)(2,1)S(1)} %copy-done.3, bf16[128,1024]{1,0:T(8,128)(2,1)S(1)} %copy-done.4, bf16[128,1024]{1,0:T(8,128)(2,1)S(1)} %copy-done.5, bf16[128,1024]{1,0:T(8,128)(2,1)S(1)} %copy-done.6, f32[2,2,1,512,256]{4,3,2,1,0:T(8,128)} %bitcast.4, ...), custom_call_target="tpu_custom_call" | custom-call | tf_op jit(solution)/shard_map/convolve/pallas_call | solution.py:544
  83.5 0.0 copy-start.1
  83.5 1.0 %copy-done.1 = f32[32,2,32,128]{3,2,1,0:T(8,128)} copy-done((f32[32,2,32,128]{3,2,1,0:T(8,128)}, f32[32,2,32,128]{3,2,1,0:T(8,128)S(1)}, u32[]{:S(2)}) %copy-start.1) | copy-done | bytes 1048600
  84.4 5.8 %finish.1 = (bf16[128,1024]{1,0:T(8,128)(2,1)}, bf16[128,1024]{1,0:T(8,128)(2,1)}, bf16[128,1024]{1,0:T(8,128)(2,1)}, bf16[128,1024]{1,0:T(8,128)(2,1)}, f32[2,2,1,512,256]{4,3,2,1,0:T(8,128)}) custom-call(bf16[128,1024]{1,0:T(8,128)(2,1)} %values.1, bf16[128,1024]{1,0:T(8,128)(2,1)} %gate_in.1, bf16[128,1024]{1,0:T(8,128)(2,1)} %gate_out.1, ...), custom_call_target="tpu_custom_call" | custom-call | tf_op jit(solution)/shard_map/finish/pallas_call | solution.py:623
Async XLA Ops:
  0.6 1.3 %copy-start = (f32[5,2,256,128]{3,2,1,0:T(8,128)S(1)}, f32[5,2,256,128]{3,2,1,0:T(8,128)}, u32[]{:S(2)}) copy-start(f32[5,2,256,128]{3,2,1,0:T(8,128)} %constant.5.clone.refs_6_) | copy-start | bytes 3932164
  2.0 1.2 %copy-start.2 = (bf16[2,512,512]{2,1,0:T(8,128)(2,1)S(1)}, bf16[2,512,512]{2,1,0:T(8,128)(2,1)}, u32[]{:S(2)}) copy-start(bf16[2,512,512]{2,1,0:T(8,128)(2,1)} %constant.4.clone.refs_5_) | copy-start | bytes 3145732
  3.2 0.9 %copy-start.3 = (bf16[128,1024]{1,0:T(8,128)(2,1)S(1)}, bf16[128,1024]{1,0:T(8,128)(2,1)}, u32[]{:S(2)}) copy-start(bf16[128,1024]{1,0:T(8,128)(2,1)} %values.1) | copy-start | bytes 786436
  4.1 0.9 %copy-start.4 = (bf16[128,1024]{1,0:T(8,128)(2,1)S(1)}, bf16[128,1024]{1,0:T(8,128)(2,1)}, u32[]{:S(2)}) copy-start(bf16[128,1024]{1,0:T(8,128)(2,1)} %gate_in.1) | copy-start | bytes 786436
  5.1 0.9 %copy-start.5 = (bf16[128,1024]{1,0:T(8,128)(2,1)S(1)}, bf16[128,1024]{1,0:T(8,128)(2,1)}, u32[]{:S(2)}) copy-start(bf16[128,1024]{1,0:T(8,128)(2,1)} %gate_out.1) | copy-start | bytes 786436
  6.0 0.9 %copy-start.6 = (bf16[128,1024]{1,0:T(8,128)(2,1)S(1)}, bf16[128,1024]{1,0:T(8,128)(2,1)}, u32[]{:S(2)}) copy-start(bf16[128,1024]{1,0:T(8,128)(2,1)} %cotangent.1) | copy-start | bytes 786436
  83.5 1.0 %copy-start.1 = (f32[32,2,32,128]{3,2,1,0:T(8,128)}, f32[32,2,32,128]{3,2,1,0:T(8,128)S(1)}, u32[]{:S(2)}) copy-start(f32[32,2,32,128]{3,2,1,0:T(8,128)S(1)} %get-tuple-element.12.found) | copy-start | bytes 3145732

commit v3 on v2

--- a/solution.py
+++ b/solution.py
@@ -142,7 +142,9 @@
         special,
         y_high,
         y_low,
-        v_work,
+        spectra,
+        filters,
+        sums,
         flipped,
         grads,
         result,
@@ -161,7 +163,7 @@
     ) = refs[9:]
     s, c = lax.axis_index("seq"), lax.axis_index("chan")
     devices = shards * groups
-    rows = source.shape[2]
+    rows = source.shape[3]
     channels = tokens.shape[2]
     width = channels // devices
     fan = LANES // width
@@ -177,6 +179,7 @@
     share = length // pack
     sets = residues(shards, fan)
     main = len(sets) - 1
+    couples = [list(range(n, min(n + 2, main + 1))) for n in range(0, main + 1, 2)]
 
     loads = [pltpu.make_async_copy(inputs[a], tokens.at[a], in_sem.at[a]) for a in range(4)]
     loads.append(pltpu.make_async_copy(matrix_in, matrix, in_sem.at[4]))
@@ -192,13 +195,13 @@
     for j, d in peers:
         pl.semaphore_signal(barrier, inc=1, device_id=(s ^ j, c ^ d), device_id_type=MESH)
 
-    def token(j, d, landing):
+    def token(sig, j, d, landing):
         to_s, to_c = (s ^ j, c ^ d) if landing else (s, c)
         return pltpu.make_async_remote_copy(
-            src_ref=source.at[(c ^ d) * shards + (s ^ j)],
-            dst_ref=held.at[to_s, to_c],
-            send_sem=t_send.at[d * shards + j],
-            recv_sem=t_recv.at[d * shards + j],
+            src_ref=source.at[sig, (c ^ d) * shards + (s ^ j)],
+            dst_ref=held.at[sig, to_s, to_c],
+            send_sem=t_send.at[sig, d * shards + j],
+            recv_sem=t_recv.at[sig, d * shards + j],
             device_id=(s ^ j, c ^ d),
             device_id_type=MESH,
         )
@@ -243,36 +246,39 @@
             device_id_type=MESH,
         )
 
-    def outcome(j, d, landing):
+    def outcome(sig, j, d, landing):
         to_s, to_c = (s ^ j, c ^ d) if landing else (s, c)
         return pltpu.make_async_remote_copy(
-            src_ref=result.at[s ^ j, c ^ d],
-            dst_ref=found.at[to_c * shards + to_s],
-            send_sem=r_send.at[d * shards + j],
-            recv_sem=r_recv.at[d * shards + j],
+            src_ref=result.at[sig, s ^ j, c ^ d],
+            dst_ref=found.at[sig, to_c * shards + to_s],
+            send_sem=r_send.at[sig, d * shards + j],
+            recv_sem=r_recv.at[sig, d * shards + j],
             device_id=(s ^ j, c ^ d),
             device_id_type=MESH,
         )
 
-    for a in range(4):
-        loads[a].wait()
-
-    def arrange(t, carry):
-        lanes = pl.ds(pl.multiple_of(t * LANES, LANES), LANES)
-        for a in range(4):
-            parts = [
-                tokens[a, g * rows : (g + 1) * rows, lanes].astype(jnp.float32)
-                for g in range(fan)
-            ]
-            for u, part in enumerate(swap_lanes(parts, width)):
-                source[t * fan + u, a] = part.astype(jnp.bfloat16)
-        return carry
-
-    lax.fori_loop(0, blocks, arrange, 0)
+    def arrange(sig):
+        for a in range(2 * sig, 2 * sig + 2):
+            loads[a].wait()
+
+        def block(t, carry):
+            lanes = pl.ds(pl.multiple_of(t * LANES, LANES), LANES)
+            for a in range(2):
+                parts = [
+                    tokens[2 * sig + a, g * rows : (g + 1) * rows, lanes].astype(jnp.float32)
+                    for g in range(fan)
+                ]
+                for u, part in enumerate(swap_lanes(parts, width)):
+                    source[sig, t * fan + u, a] = part.astype(jnp.bfloat16)
+            return carry
+
+        lax.fori_loop(0, blocks, block, 0)
+
+    arrange(0)
     pl.semaphore_wait(barrier, len(peers))
     for j, d in peers:
-        token(j, d, False).start()
-
+        token(0, j, d, False).start()
+    arrange(1)
     for load in loads[6:]:
         load.wait()
     wide = raw.shape[4]
@@ -302,12 +308,19 @@
         return carry
 
     lax.fori_loop(0, raw.shape[0] * STEPS, arrange_filter, 0)
-    for j in range(1, shards):
-        spectrum(j, False).start()
+    pending = list(range(1, shards))
+    every = len(peers) // len(pending)
+    for i, (j, d) in enumerate(peers):
+        token(1, j, d, False).start()
+        if pending and i % every == 0:
+            spectrum(pending.pop(0), False).start()
     own = [
-        pltpu.make_async_copy(source.at[c * shards + s], held.at[s, c], own_sem.at[0]),
-        pltpu.make_async_copy(hsrc.at[s], hheld.at[s], own_sem.at[1]),
+        pltpu.make_async_copy(
+            source.at[sig, c * shards + s], held.at[sig, s, c], own_sem.at[sig]
+        )
+        for sig in range(2)
     ]
+    own.append(pltpu.make_async_copy(hsrc.at[s], hheld.at[s], own_sem.at[2]))
     for copy in own:
         copy.start()
 
@@ -315,29 +328,32 @@
     def _():
         for j in range(1, shards):
             extra(j).start()
-        copy = pltpu.make_async_copy(hspec.at[0], special, own_sem.at[2])
+        copy = pltpu.make_async_copy(hspec.at[0], special, own_sem.at[3])
         copy.start()
         copy.wait()
 
-    own[0].wait()
-    for j, d in peers:
-        token(j, d, True).wait_recv()
+    def arrived(sig):
+        own[sig].wait()
+        for j, d in peers:
+            token(sig, j, d, True).wait_recv()
+
+    arrived(0)
     loads[4].wait()
     loads[5].wait()
 
     def zero():
         return jnp.zeros((step, LANES), jnp.float32)
 
-    def forward(k, carry):
-        c1, piece = k // chunks, k % chunks
-        here = pl.ds(pl.multiple_of(piece * step, step), step)
-        for sig in range(2):
+    def forward(sig):
+        def chunk(k, carry):
+            c1, piece = k // chunks, k % chunks
+            here = pl.ds(pl.multiple_of(piece * step, step), step)
             values = []
             for b in range(2 * shards):
-                block = held.at[b // 2, (b % 2) * near + c1]
-                left = block[0 if sig == 0 else 3, here].astype(jnp.float32)
-                right = block[1 if sig == 0 else 2, here].astype(jnp.float32)
-                values.append(left * right)
+                block = held.at[sig, b // 2, (b % 2) * near + c1]
+                values.append(
+                    block[0, here].astype(jnp.float32) * block[1, here].astype(jnp.float32)
+                )
             ladder = forward_ladder(values)
             for n, slots in enumerate(sets):
                 sides = []
@@ -346,22 +362,71 @@
                     sides.append(
                         swap_lanes([zero() if a is None else a for a in arrays], width)
                     )
+                lanes = slice(n % 2 * LANES, (n % 2 + 1) * LANES)
                 for g in range(fan):
                     at = pl.multiple_of(c1 * spread + g * rows + piece * step, step)
                     spot = pl.ds(at, step)
                     cos, sin = twiddle[n, 0, spot, :], twiddle[n, 1, spot, :]
                     real, imag = sides[0][g], sides[1][g]
                     high, low = halves(real * cos + imag * sin)
-                    lanes = slice(sig * LANES, (sig + 1) * LANES)
-                    y_high[n, spot, lanes] = high
-                    y_low[n, spot, lanes] = low
+                    y_high[n // 2, spot, lanes] = high
+                    y_low[n // 2, spot, lanes] = low
                     high, low = halves(imag * cos - real * sin)
                     spot = pl.ds(pl.multiple_of(length + at, step), step)
-                    y_high[n, spot, lanes] = high
-                    y_low[n, spot, lanes] = low
-        return carry
-
-    lax.fori_loop(0, near * chunks, forward, 0)
+                    y_high[n // 2, spot, lanes] = high
+                    y_low[n // 2, spot, lanes] = low
+            return carry
+
+        lax.fori_loop(0, near * chunks, chunk, 0)
+
+    def analyse(sig, m):
+        lanes = slice(0, len(couples[m]) * LANES)
+        both = transform(matrix, y_high[m, :, lanes], y_low[m, :, lanes])
+        spectra[sig, m, 0, :, lanes] = both[:length]
+        spectra[sig, m, 1, :, lanes] = both[length:]
+
+    def tables(m):
+        return [
+            jnp.concatenate([twiddle[n, p] for n in couples[m]], axis=1) for p in range(2)
+        ]
+
+    def synthesise(sig, m):
+        lanes = slice(0, len(couples[m]) * LANES)
+        fr, fi = filters[m, 0, :, lanes], filters[m, 1, :, lanes]
+        real, imag = spectra[sig, m, 0, :, lanes], spectra[sig, m, 1, :, lanes]
+        if sig == 0:
+            stacked = [real * fr - imag * fi, -(real * fi + imag * fr)]
+        else:
+            stacked = [real * fr + imag * fi, real * fi - imag * fr]
+        high, low = halves(jnp.concatenate(stacked, axis=0))
+        both = transform(matrix, high, low)
+        cos, sin = tables(m)
+        real, against = both[:length], both[length:]
+        sums[m, 0, :, lanes] = real * cos + against * sin
+        sums[m, 1, :, lanes] = real * sin - against * cos
+
+    def inverse(sig):
+        def chunk(k, carry):
+            c1, piece = k // chunks, k % chunks
+            here = pl.ds(pl.multiple_of(piece * step, step), step)
+            values = [[None, None] for _ in range(2 * shards + 1)]
+            for n, slots in enumerate(sets):
+                lanes = slice(n % 2 * LANES, (n % 2 + 1) * LANES)
+                for p in range(2):
+                    arrays = []
+                    for g in range(fan):
+                        at = pl.multiple_of(c1 * spread + g * rows + piece * step, step)
+                        arrays.append(sums[n // 2, p, pl.ds(at, step), lanes])
+                    for f, array in zip(slots, swap_lanes(arrays, width)):
+                        if f is not None:
+                            values[f][p] = array
+            for b, value in enumerate(inverse_ladder([tuple(v) for v in values])):
+                result[sig, b // 2, (b % 2) * near + c1, here, :] = value
+            return carry
+
+        lax.fori_loop(0, near * chunks, chunk, 0)
+        for j, d in peers:
+            outcome(sig, j, d, False).start()
 
     flip = (
         lax.broadcasted_iota(jnp.int32, (length, length), 0)
@@ -386,11 +451,54 @@
         def _():
             slope(odd, r).start()
 
+    forward(0)
+    for m in range(len(couples)):
+        analyse(0, m)
+
+    own[2].wait()
+    for j in range(1, shards):
+        spectrum(j, True).wait_recv()
+
+    @pl.when(s != 0)
+    def _():
+        extra(s).wait_recv()
+
     for n in range(main + 1):
-        spectra = transform(matrix, y_high[n], y_low[n])
-        v_work[n, 0], v_work[n, 1] = spectra[:length], spectra[length:]
-        sr, cr = spectra[:length, :LANES], spectra[:length, LANES:]
-        si, ci = spectra[length:, :LANES], spectra[length:, LANES:]
+        if n < main:
+            arrays = swap_lanes([hheld[r] for r in members(n)], 2 * width)
+            fr = jnp.concatenate(arrays[0::2], axis=0)
+            fi = jnp.concatenate(arrays[1::2], axis=0)
+        else:
+            small = length // 4 // 2 // pack
+            pieces = [[], []]
+            for q in range(pack):
+                for t in range(STEPS):
+                    for half in range(2):
+                        block = special[t * small : (t + 1) * small]
+                        for p in range(2):
+                            shift = ((q * 2 + half) * 2 + p) * width
+                            moved = pltpu.roll(block, LANES - shift, 1) if shift else block
+                            pieces[p].append(jnp.where(first, moved, 0.0))
+            fr, fi = (jnp.concatenate(piece, axis=0) for piece in pieces)
+        weight = jnp.full((1, LANES), 2.0 / total, jnp.float32)
+        if None in sets[n] or 0 in sets[n]:
+            weight = jnp.where(first, 1.0 / total, weight)
+        lanes = slice(n % 2 * LANES, (n % 2 + 1) * LANES)
+        filters[n // 2, 0, :, lanes] = fr * weight
+        filters[n // 2, 1, :, lanes] = fi * weight
+
+    for m in range(len(couples)):
+        synthesise(0, m)
+    inverse(0)
+
+    arrived(1)
+    forward(1)
+    for n in range(main + 1):
+        if n % 2 == 0:
+            analyse(1, n // 2)
+        lanes = slice(n % 2 * LANES, (n % 2 + 1) * LANES)
+        sr, si = (spectra[0, n // 2, p, :, lanes] for p in range(2))
+        cr, ci = (spectra[1, n // 2, p, :, lanes] for p in range(2))
         slope_real = (sr * cr + si * ci) * (1.0 / total)
         slope_imag = (sr * ci - si * cr) * (1.0 / total)
         if n < main:
@@ -421,89 +529,26 @@
         near_even = flipped[mirrored(shards - place, bits)] if place else last
         grads[1, r] = jnp.where(even_lane, near_even, flipped[shards - 1 - r])
 
-    own[1].wait()
-    for j in range(1, shards):
-        spectrum(j, True).wait_recv()
-
-    @pl.when(s != 0)
-    def _():
-        extra(s).wait_recv()
-
-    for n in range(main + 1):
-        if n < main:
-            filters = swap_lanes([hheld[r] for r in members(n)], 2 * width)
-            fr = jnp.concatenate(filters[0::2], axis=0)
-            fi = jnp.concatenate(filters[1::2], axis=0)
-        else:
-            small = length // 4 // 2 // pack
-            pieces = [[], []]
-            for q in range(pack):
-                for t in range(STEPS):
-                    for half in range(2):
-                        block = special[t * small : (t + 1) * small]
-                        for p in range(2):
-                            shift = ((q * 2 + half) * 2 + p) * width
-                            moved = pltpu.roll(block, LANES - shift, 1) if shift else block
-                            pieces[p].append(jnp.where(first, moved, 0.0))
-            fr, fi = (jnp.concatenate(piece, axis=0) for piece in pieces)
-        weight = jnp.full((1, LANES), 2.0 / total, jnp.float32)
-        if None in sets[n] or 0 in sets[n]:
-            weight = jnp.where(first, 1.0 / total, weight)
-        fr, fi = fr * weight, fi * weight
-        sr, cr = v_work[n, 0, :, :LANES], v_work[n, 0, :, LANES:]
-        si, ci = v_work[n, 1, :, :LANES], v_work[n, 1, :, LANES:]
-        stacked = jnp.concatenate(
-            [
-                jnp.concatenate([sr * fr - si * fi, cr * fr + ci * fi], axis=1),
-                jnp.concatenate([-(sr * fi + si * fr), cr * fi - ci * fr], axis=1),
-            ],
-            axis=0,
-        )
-        high, low = halves(stacked)
-        sums = transform(matrix, high, low)
-        cos = jnp.concatenate([twiddle[n, 0]] * 2, axis=1)
-        sin = jnp.concatenate([twiddle[n, 1]] * 2, axis=1)
-        real, against = sums[:length], sums[length:]
-        v_work[n, 0] = real * cos + against * sin
-        v_work[n, 1] = real * sin - against * cos
-        if n == 0:
+    for m in range(len(couples)):
+        synthesise(1, m)
+        if m == 0:
             for r in range(shards):
                 send(1, r)
-
     mine = [
-        pltpu.make_async_copy(grads.at[odd, s], landed.at[odd, s], own_sem.at[3 + odd])
+        pltpu.make_async_copy(grads.at[odd, s], landed.at[odd, s], own_sem.at[4 + odd])
         for odd in range(2)
     ]
     for copy in mine:
         copy.start()
-
-    def inverse(k, carry):
-        c1, piece = k // chunks, k % chunks
-        here = pl.ds(pl.multiple_of(piece * step, step), step)
-        for sig in range(2):
-            values = [[None, None] for _ in range(2 * shards + 1)]
-            for n, slots in enumerate(sets):
-                for p in range(2):
-                    arrays = []
-                    for g in range(fan):
-                        at = pl.multiple_of(c1 * spread + g * rows + piece * step, step)
-                        lanes = slice(sig * LANES, (sig + 1) * LANES)
-                        arrays.append(v_work[n, p, pl.ds(at, step), lanes])
-                    for f, array in zip(slots, swap_lanes(arrays, width)):
-                        if f is not None:
-                            values[f][p] = array
-            for b, value in enumerate(inverse_ladder([tuple(v) for v in values])):
-                result[b // 2, (b % 2) * near + c1, sig, here, :] = value
-        return carry
-
-    lax.fori_loop(0, near * chunks, inverse, 0)
-    for j, d in peers:
-        outcome(j, d, False).start()
-    rest = pltpu.make_async_copy(result.at[s, c], found.at[c * shards + s], own_sem.at[5])
+    inverse(1)
+    rest = pltpu.make_async_copy(
+        result.at[:, s, c], found.at[:, c * shards + s], own_sem.at[6]
+    )
     rest.start()
 
-    for j, d in peers:
-        token(j, d, False).wait_send()
+    for sig in range(2):
+        for j, d in peers:
+            token(sig, j, d, False).wait_send()
     for j in range(1, shards):
         spectrum(j, False).wait_send()
 
@@ -522,10 +567,11 @@
                 arrival(odd, r).wait_recv()
                 slope(odd, r).wait_send()
 
-    for j, d in peers:
-        outcome(j, d, True).wait_recv()
-    for j, d in peers:
-        outcome(j, d, False).wait_send()
+    for sig in range(2):
+        for j, d in peers:
+            outcome(sig, j, d, True).wait_recv()
+        for j, d in peers:
+            outcome(sig, j, d, False).wait_send()
 
 
 def convolve(inputs, filt, tables, shards, groups):
@@ -538,13 +584,14 @@
     matrix, twiddle = tables
     sets, _, length, _ = twiddle.shape
     share = length // pack
+    couples = (sets + 1) // 2
     raw = filt.reshape(2, 2, pack, 2 * share, filt.shape[4])
     dma, vmem = pltpu.SemaphoreType.DMA, pltpu.VMEM
     f32, bf16 = jnp.float32, jnp.bfloat16
     return pl.pallas_call(
         functools.partial(convolve_kernel, shards, groups),
         out_shape=(
-            jax.ShapeDtypeStruct((devices, 2, short, LANES), f32),
+            jax.ShapeDtypeStruct((2, devices, short, LANES), f32),
             jax.ShapeDtypeStruct((2, shards, share, LANES), f32),
         ),
         in_specs=[ANY] * 7,
@@ -554,33 +601,35 @@
             vmem((raw.shape[4] // LANES,) + raw.shape[:4] + (LANES,), f32),
             vmem(matrix.shape, bf16),
             vmem(twiddle.shape, f32),
-            vmem((devices, 4, short, LANES), bf16),
+            vmem((2, devices, 2, short, LANES), bf16),
             vmem((shards, share, LANES), f32),
             vmem((shards, share // 2, LANES), f32),
-            vmem((shards, groups, 4, short, LANES), bf16),
+            vmem((2, shards, groups, 2, short, LANES), bf16),
             vmem((shards, share, LANES), f32),
             vmem((share // 2, LANES), f32),
-            vmem((sets, 2 * length, 2 * LANES), bf16),
-            vmem((sets, 2 * length, 2 * LANES), bf16),
-            vmem((sets, 2, length, 2 * LANES), f32),
+            vmem((couples, 2 * length, 2 * LANES), bf16),
+            vmem((couples, 2 * length, 2 * LANES), bf16),
+            vmem((2, couples, 2, length, 2 * LANES), f32),
+            vmem((couples, 2, length, 2 * LANES), f32),
+            vmem((couples, 2, length, 2 * LANES), f32),
             vmem((shards, share, LANES), f32),
             vmem((2, shards, share, LANES), f32),
-            vmem((shards, groups, 2, short, LANES), f32),
+            vmem((2, shards, groups, short, LANES), f32),
             dma((6 + raw.shape[4] // LANES,)),
-            dma((6,)),
-            dma((devices,)),
-            dma((devices,)),
+            dma((7,)),
+            dma((2, devices)),
+            dma((2, devices)),
             dma((shards,)),
             dma((shards,)),
             dma((shards,)),
             dma,
             dma((2, shards)),
             dma((2, shards)),
-            dma((devices,)),
-            dma((devices,)),
+            dma((2, devices)),
+            dma((2, devices)),
         ],
         compiler_params=pltpu.CompilerParams(
-            collective_id=0, has_side_effects=True, vmem_limit_bytes=48 * 1024 * 1024
+            collective_id=0, has_side_effects=True, vmem_limit_bytes=63 * 1024 * 1024
         ),
         name="convolve",
     )(*inputs, raw, matrix, twiddle)
@@ -589,10 +638,11 @@
 def finish_kernel(width, values, gate_in, gate_out, cotangent, found, landed, *outs):
     rows = found.shape[2]
     fan = landed.shape[1]
-    for block in range(found.shape[0] // fan):
-        parts = [found.at[block * fan + u] for u in range(fan)]
-        conv = swap_lanes([part[0] for part in parts], width)
-        back = swap_lanes([part[1] for part in parts], width)
+    for block in range(found.shape[1] // fan):
+        conv, back = (
+            swap_lanes([found[sig, block * fan + u] for u in range(fan)], width)
+            for sig in range(2)
+        )
         lanes = slice(block * LANES, (block + 1) * LANES)
         for g in range(fan):
             here = slice(g * rows, (g + 1) * rows)
@@ -612,7 +662,7 @@
 
 def finish(inputs, found, landed, filt):
     rows, channels = inputs[0].shape
-    devices, _, short, _ = found.shape
+    _, devices, short, _ = found.shape
     width = channels // devices
     fan = LANES // width
     pack = fan // 4
@@ -627,7 +677,7 @@
         + (jax.ShapeDtypeStruct((2, 2, pack, 2 * share, filt.shape[4]), jnp.float32),),
         in_specs=[column] * 4
         + [
-            pl.BlockSpec((tiles * fan, 2, short, LANES), lambda t: (t, 0, 0, 0)),
+            pl.BlockSpec((2, tiles * fan, short, LANES), lambda t: (0, t, 0, 0)),
             pl.BlockSpec(
                 (2, fan, share // pieces, LANES), lambda t: (0, t // pieces, t % pieces, 0)
             ),

time: 90.6 us -> 85 us (0.938)
  local copies, waits for them, and re-layouts: 7.31 us -> 0 us
  Pallas kernels: 82.2 us -> 84.2 us
    unnamed x14 -> x0, local copies, waits for them, and re-layouts: 7.31 us -> none
    pallas_call x1, Pallas kernels: 76.5 us -> 78.4 us  [convolve(): pl.pallas_call(functools.partial(convolve_kernel, shards, groups), out_sh...]
where the time goes in v3:
time: 85 us; the launch traced here: 84.8 us
  Pallas kernels  84.2 us (99%)
    pallas_call x1, Pallas kernels, convolve(): pl.pallas_call(functools.partial(convolve_kernel, shards, groups), out_sh...  78.4 us
    pallas_call x1, Pallas kernels, finish(): pl.pallas_call(functools.partial(finish_kernel, width), grid=(STEPS,), ou...  5.8 us

profile of v3, /device:TPU:0, one launch (start us, length us, event | category | flops | bytes accessed | tf_op | source)
XLA Modules:
  0.0 84.8 jit_solution(13600373003995515526)
XLA Ops:
  0.6 78.4 %convolve.1 = (f32[2,32,32,128]{3,2,1,0:T(8,128)}, f32[2,8,256,128]{3,2,1,0:T(8,128)}) custom-call(bf16[128,1024]{1,0:T(8,128)(2,1)} %values.1, bf16[128,1024]{1,0:T(8,128)(2,1)} %gate_in.1, bf16[128,1024]{1,0:T(8,128)(2,1)} %gate_out.1, bf16[128,1024]{1,0:T(8,128)(2,1)} %cotangent.1, f32[2,2,1,512,256]{4,3,2,1,0:T(8,128)} %bitcast.4, ...), custom_call_target="tpu_custom_call" | custom-call | tf_op jit(solution)/shard_map/convolve/pallas_call | solution.py:591
  79.0 5.8 %finish.1 = (bf16[128,1024]{1,0:T(8,128)(2,1)}, bf16[128,1024]{1,0:T(8,128)(2,1)}, bf16[128,1024]{1,0:T(8,128)(2,1)}, bf16[128,1024]{1,0:T(8,128)(2,1)}, f32[2,2,1,512,256]{4,3,2,1,0:T(8,128)}) custom-call(bf16[128,1024]{1,0:T(8,128)(2,1)} %values.1, bf16[128,1024]{1,0:T(8,128)(2,1)} %gate_in.1, bf16[128,1024]{1,0:T(8,128)(2,1)} %gate_out.1, ...), custom_call_target="tpu_custom_call" | custom-call | tf_op jit(solution)/shard_map/finish/pallas_call | solution.py:673

commit v4 on v3

--- a/solution.py
+++ b/solution.py
@@ -113,6 +113,24 @@
     return out
 
 
+def encode(data):
+    largest = jnp.max(jnp.abs(data), axis=0, keepdims=True).astype(jnp.bfloat16)
+    wide = largest.astype(jnp.float32)
+    ratio = data * jnp.where(wide > 2.0**-110, 2.0**15 / jnp.maximum(wide, 2.0**-110), 0.0)
+    square = ratio * ratio
+    fourth = square * square
+    eighth = fourth * fourth
+    return jnp.where(ratio < 0.0, -eighth, eighth).astype(jnp.bfloat16), wide
+
+
+def decode(code, largest):
+    code = code.astype(jnp.float32)
+    size = jnp.abs(code)
+    root = jnp.exp2(jnp.log2(jnp.maximum(size, 2.0**-126)) * 0.125)
+    root = jnp.where(size >= 2.0**-126, root, 0.0) * (largest * 2.0**-15)
+    return jnp.where(code < 0.0, -root, root)
+
+
 def residues(shards, fan):
     bits = shards.bit_length() - 1
     flat = [2 * mirrored(r, bits) + e for r in range(shards) for e in range(2)]
@@ -128,7 +146,7 @@
 
 
 def convolve_kernel(shards, groups, *refs):
-    inputs, filt, matrix_in, twiddle_in, found, landed = refs[:4], *refs[4:9]
+    inputs, filt, matrix_in, twiddle_in, found, slopes = refs[:4], *refs[4:9]
     (
         tokens,
         raw,
@@ -147,6 +165,8 @@
         sums,
         flipped,
         grads,
+        landed,
+        gathered,
         result,
         in_sem,
         own_sem,
@@ -190,7 +210,7 @@
     for load in loads:
         load.start()
 
-    peers = [(j, d) for d in range(groups - 1, -1, -1) for j in range(shards) if j or d]
+    peers = [(j, d) for d in range(groups) for j in range(shards) if j or d]
     barrier = pltpu.get_barrier_semaphore()
     for j, d in peers:
         pl.semaphore_signal(barrier, inc=1, device_id=(s ^ j, c ^ d), device_id_type=MESH)
@@ -218,7 +238,7 @@
 
     def extra(j):
         return pltpu.make_async_remote_copy(
-            src_ref=hspec.at[j],
+            src_ref=hspec.at[j, pl.ds(0, share // 4)],
             dst_ref=special,
             send_sem=x_send.at[j],
             recv_sem=x_recv,
@@ -309,11 +329,10 @@
 
     lax.fori_loop(0, raw.shape[0] * STEPS, arrange_filter, 0)
     pending = list(range(1, shards))
-    every = len(peers) // len(pending)
-    for i, (j, d) in enumerate(peers):
+    for j, d in peers:
         token(1, j, d, False).start()
-        if pending and i % every == 0:
-            spectrum(pending.pop(0), False).start()
+    for j in pending:
+        spectrum(j, False).start()
     own = [
         pltpu.make_async_copy(
             source.at[sig, c * shards + s], held.at[sig, s, c], own_sem.at[sig]
@@ -328,7 +347,9 @@
     def _():
         for j in range(1, shards):
             extra(j).start()
-        copy = pltpu.make_async_copy(hspec.at[0], special, own_sem.at[3])
+        copy = pltpu.make_async_copy(
+            hspec.at[0, pl.ds(0, share // 4)], special, own_sem.at[3]
+        )
         copy.start()
         copy.wait()
 
@@ -446,6 +467,11 @@
     def members(n):
         return [n * (fan // 2) + i for i in range(fan // 2)] if n < main else []
 
+    def post(odd, r, data):
+        code, largest = encode(data)
+        grads[odd, r, :share] = code
+        grads[odd, r, share:] = jnp.broadcast_to(largest, (16, LANES)).astype(jnp.bfloat16)
+
     def send(odd, r):
         @pl.when(s != r)
         def _():
@@ -474,6 +500,10 @@
             for q in range(pack):
                 for t in range(STEPS):
                     for half in range(2):
+                        if t >= STEPS // 2:
+                            for p in range(2):
+                                pieces[p].append(jnp.zeros((small, LANES), jnp.float32))
+                            continue
                         block = special[t * small : (t + 1) * small]
                         for p in range(2):
                             shift = ((q * 2 + half) * 2 + p) * width
@@ -481,7 +511,7 @@
                             pieces[p].append(jnp.where(first, moved, 0.0))
             fr, fi = (jnp.concatenate(piece, axis=0) for piece in pieces)
         weight = jnp.full((1, LANES), 2.0 / total, jnp.float32)
-        if None in sets[n] or 0 in sets[n]:
+        if 0 in sets[n]:
             weight = jnp.where(first, 1.0 / total, weight)
         lanes = slice(n % 2 * LANES, (n % 2 + 1) * LANES)
         filters[n // 2, 0, :, lanes] = fr * weight
@@ -503,7 +533,7 @@
         slope_imag = (sr * ci - si * cr) * (1.0 / total)
         if n < main:
             for r, part in zip(members(n), packets(slope_real, slope_imag)):
-                grads[0, r] = part
+                post(0, r, part)
             high, low = halves(jnp.concatenate([slope_real, slope_imag], axis=1))
             turned_over = jnp.dot(flip, high, preferred_element_type=jnp.float32) + jnp.dot(
                 flip, low, preferred_element_type=jnp.float32
@@ -527,7 +557,7 @@
     for r in range(shards):
         place = mirrored(r, bits)
         near_even = flipped[mirrored(shards - place, bits)] if place else last
-        grads[1, r] = jnp.where(even_lane, near_even, flipped[shards - 1 - r])
+        post(1, r, jnp.where(even_lane, near_even, flipped[shards - 1 - r]))
 
     for m in range(len(couples)):
         synthesise(1, m)
@@ -546,6 +576,43 @@
     )
     rest.start()
 
+    for copy in mine:
+        copy.wait()
+    for odd in range(2):
+        for r in range(shards):
+
+            @pl.when(s != r)
+            def _():
+                arrival(odd, r).wait_recv()
+
+    tall = share // STEPS
+
+    def gather(t, carry):
+        column, piece = t // STEPS, t % STEPS
+        for odd in range(2):
+            arrays = []
+            for u in range(fan):
+                block = landed.at[odd, column * fan + u]
+                largest = block[share : share + 16].astype(jnp.float32)[0:1]
+                at = pl.ds(pl.multiple_of(piece * tall, tall), tall)
+                arrays.append(decode(block[at], largest))
+            for i, slope_part in enumerate(swap_lanes(arrays, width)):
+                at = pl.ds(2 * tall * piece + odd, tall, stride=2)
+                gathered[column, i // 2 % 2, i % 2, i // 4, at, :] = slope_part
+        return carry
+
+    lax.fori_loop(0, gathered.shape[0] * STEPS, gather, 0)
+    stores = [
+        pltpu.make_async_copy(
+            gathered.at[i],
+            slopes.at[:, :, :, :, pl.ds(i * LANES, LANES)],
+            own_sem.at[7 + i],
+        )
+        for i in range(gathered.shape[0])
+    ]
+    for store in stores:
+        store.start()
+
     for sig in range(2):
         for j, d in peers:
             token(sig, j, d, False).wait_send()
@@ -557,16 +624,15 @@
         for j in range(1, shards):
             extra(j).wait_send()
 
-    for copy in mine + [rest]:
-        copy.wait()
     for odd in range(2):
         for r in range(shards):
 
             @pl.when(s != r)
             def _():
-                arrival(odd, r).wait_recv()
                 slope(odd, r).wait_send()
 
+    for copy in stores + [rest]:
+        copy.wait()
     for sig in range(2):
         for j, d in peers:
             outcome(sig, j, d, True).wait_recv()
@@ -592,7 +658,7 @@
         functools.partial(convolve_kernel, shards, groups),
         out_shape=(
             jax.ShapeDtypeStruct((2, devices, short, LANES), f32),
-            jax.ShapeDtypeStruct((2, shards, share, LANES), f32),
+            jax.ShapeDtypeStruct(raw.shape, f32),
         ),
         in_specs=[ANY] * 7,
         out_specs=(ANY, ANY),
@@ -606,17 +672,19 @@
             vmem((shards, share // 2, LANES), f32),
             vmem((2, shards, groups, 2, short, LANES), bf16),
             vmem((shards, share, LANES), f32),
-            vmem((share // 2, LANES), f32),
+            vmem((share // 4, LANES), f32),
             vmem((couples, 2 * length, 2 * LANES), bf16),
             vmem((couples, 2 * length, 2 * LANES), bf16),
             vmem((2, couples, 2, length, 2 * LANES), f32),
             vmem((couples, 2, length, 2 * LANES), f32),
             vmem((couples, 2, length, 2 * LANES), f32),
             vmem((shards, share, LANES), f32),
-            vmem((2, shards, share, LANES), f32),
+            vmem((2, shards, share + 16, LANES), bf16),
+            vmem((2, shards, share + 16, LANES), bf16),
+            vmem((raw.shape[4] // LANES,) + raw.shape[:4] + (LANES,), f32),
             vmem((2, shards, groups, short, LANES), f32),
             dma((6 + raw.shape[4] // LANES,)),
-            dma((7,)),
+            dma((7 + raw.shape[4] // LANES,)),
             dma((2, devices)),
             dma((2, devices)),
             dma((shards,)),
@@ -635,9 +703,8 @@
     )(*inputs, raw, matrix, twiddle)
 
 
-def finish_kernel(width, values, gate_in, gate_out, cotangent, found, landed, *outs):
+def finish_kernel(width, fan, values, gate_in, gate_out, cotangent, found, *outs):
     rows = found.shape[2]
-    fan = landed.shape[1]
     for block in range(found.shape[1] // fan):
         conv, back = (
             swap_lanes([found[sig, block * fan + u] for u in range(fan)], width)
@@ -654,44 +721,24 @@
             outs[1][here, lanes] = (back[g] * wide(gate_in)).astype(jnp.bfloat16)
             outs[2][here, lanes] = (back[g] * wide(values)).astype(jnp.bfloat16)
             outs[3][here, lanes] = (wide(cotangent) * conv[g]).astype(jnp.bfloat16)
-    span = landed.shape[2]
-    for odd in range(2):
-        for i, slope in enumerate(swap_lanes([landed[odd, u] for u in range(fan)], width)):
-            outs[4][i // 2 % 2, i % 2, i // 4, pl.ds(odd, span, stride=2), :] = slope
-
-
-def finish(inputs, found, landed, filt):
+
+
+def finish(inputs, found):
     rows, channels = inputs[0].shape
     _, devices, short, _ = found.shape
     width = channels // devices
     fan = LANES // width
-    pack = fan // 4
-    share = landed.shape[2]
     tiles = channels // LANES // STEPS
     column = pl.BlockSpec((rows, tiles * LANES), lambda t: (0, t))
-    pieces = STEPS * LANES // filt.shape[4]
-    outs = pl.pallas_call(
-        functools.partial(finish_kernel, width),
+    return pl.pallas_call(
+        functools.partial(finish_kernel, width, fan),
         grid=(STEPS,),
-        out_shape=tuple(jax.ShapeDtypeStruct((rows, channels), jnp.bfloat16) for _ in range(4))
-        + (jax.ShapeDtypeStruct((2, 2, pack, 2 * share, filt.shape[4]), jnp.float32),),
+        out_shape=tuple(jax.ShapeDtypeStruct((rows, channels), jnp.bfloat16) for _ in range(4)),
         in_specs=[column] * 4
-        + [
-            pl.BlockSpec((2, tiles * fan, short, LANES), lambda t: (0, t, 0, 0)),
-            pl.BlockSpec(
-                (2, fan, share // pieces, LANES), lambda t: (0, t // pieces, t % pieces, 0)
-            ),
-        ],
-        out_specs=(column,) * 4
-        + (
-            pl.BlockSpec(
-                (2, 2, pack, 2 * share // pieces, LANES),
-                lambda t: (0, 0, 0, t % pieces, t // pieces),
-            ),
-        ),
+        + [pl.BlockSpec((2, tiles * fan, short, LANES), lambda t: (0, t, 0, 0))],
+        out_specs=(column,) * 4,
         name="finish",
-    )(*inputs, found, landed)
-    return outs[:4] + (outs[4].reshape(filt.shape),)
+    )(*inputs, found)
 
 
 def make_tables(shards, fan, length):
@@ -716,8 +763,8 @@
     rows, channels = values_in.shape
     fan = LANES * shards * groups // channels
     tables = make_tables(shards, fan, rows * groups // 2)
-    found, landed = convolve(inputs, filter_spectra, tables, shards, groups)
-    return finish(inputs, found, landed, filter_spectra)
+    found, slopes = convolve(inputs, filter_spectra, tables, shards, groups)
+    return tuple(finish(inputs, found)) + (slopes.reshape(filter_spectra.shape),)
 
 
 def solution(mesh):

time: 85 us -> 73.9 us (0.87); the launches traced: 84.8 us -> 72.5 us
  Pallas kernels: 84.2 us -> 70.5 us
  local copies, waits for them, and re-layouts: 0 us -> 1.33 us
    pallas_call x1, Pallas kernels: 78.4 us -> 66.3 us  [convolve(): pl.pallas_call(functools.partial(convolve_kernel, shards, groups), out_sh...]
    pallas_call x1, Pallas kernels: 5.8 us -> 4.24 us  [finish(): pl.pallas_call(functools.partial(finish_kernel, width, fan), grid=(STEPS,...]
    unnamed x0 -> x3, local copies, waits for them, and re-layouts: none -> 1.33 us
where the time goes in v4:
time: 73.9 us; the launch traced here: 72.5 us
  Pallas kernels  70.5 us (95%)
  local copies, waits for them, and re-layouts  1.33 us (2%)
    pallas_call x1, Pallas kernels, convolve(): pl.pallas_call(functools.partial(convolve_kernel, shards, groups), out_sh...  66.3 us
    pallas_call x1, Pallas kernels, finish(): pl.pallas_call(functools.partial(finish_kernel, width, fan), grid=(STEPS,...  4.24 us

profile of v4, /device:TPU:0, one launch (start us, length us, event | category | flops | bytes accessed | tf_op | source)
XLA Modules:
  0.0 72.5 jit_solution(12616574673478297399)
XLA Ops:
  0.6 66.3 %convolve.1 = (f32[2,32,32,128]{3,2,1,0:T(8,128)}, f32[2,2,1,512,256]{4,3,2,1,0:T(8,128)}) custom-call(bf16[128,1024]{1,0:T(8,128)(2,1)} %values.1, bf16[128,1024]{1,0:T(8,128)(2,1)} %gate_in.1, bf16[128,1024]{1,0:T(8,128)(2,1)} %gate_out.1, bf16[128,1024]{1,0:T(8,128)(2,1)} %cotangent.1, f32[2,2,1,512,256]{4,3,2,1,0:T(8,128)} %bitcast.4, ...), custom_call_target="tpu_custom_call" | custom-call | tf_op jit(solution)/shard_map/convolve/pallas_call | solution.py:657
  66.9 0.0 copy-start
  66.9 4.2 %finish.1 = (bf16[128,1024]{1,0:T(8,128)(2,1)}, bf16[128,1024]{1,0:T(8,128)(2,1)}, bf16[128,1024]{1,0:T(8,128)(2,1)}, bf16[128,1024]{1,0:T(8,128)(2,1)}) custom-call(bf16[128,1024]{1,0:T(8,128)(2,1)} %values.1, bf16[128,1024]{1,0:T(8,128)(2,1)} %gate_in.1, bf16[128,1024]{1,0:T(8,128)(2,1)} %gate_out.1, bf16[128,1024]{1,0:T(8,128)(2,1)} %cotangent.1, ...), custom_call_target="tpu_custom_call" | custom-call | tf_op jit(solution)/shard_map/finish/pallas_call | solution.py:733
  71.2 0.0 copy-done
  71.2 1.3 %copy.14 = f32[2,1,2,512,256]{4,3,2,1,0:T(8,128)} copy(f32[2,1,2,512,256]{4,3,2,1,0:T(8,128)S(1)} %bitcast.5) | data formatting | bytes 4194304
Async XLA Ops:
  66.9 4.2 %copy-start = (f32[2,2,1,512,256]{4,3,2,1,0:T(8,128)S(1)}, f32[2,2,1,512,256]{4,3,2,1,0:T(8,128)}, u32[]{:S(2)}) copy-start(f32[2,2,1,512,256]{4,3,2,1,0:T(8,128)} %get-tuple-element.16) | copy-start | bytes 6291460

commit v5 on v4

--- a/solution.py
+++ b/solution.py
@@ -329,10 +329,11 @@
 
     lax.fori_loop(0, raw.shape[0] * STEPS, arrange_filter, 0)
     pending = list(range(1, shards))
-    for j, d in peers:
-        token(1, j, d, False).start()
     for j in pending:
         spectrum(j, False).start()
+    for j, d in peers:
+        if j < 2:
+            token(1, j, d, False).start()
     own = [
         pltpu.make_async_copy(
             source.at[sig, c * shards + s], held.at[sig, s, c], own_sem.at[sig]
@@ -359,6 +360,9 @@
             token(sig, j, d, True).wait_recv()
 
     arrived(0)
+    for j, d in peers:
+        if j >= 2:
+            token(1, j, d, False).start()
     loads[4].wait()
     loads[5].wait()
 
@@ -576,20 +580,18 @@
     )
     rest.start()
 
-    for copy in mine:
-        copy.wait()
-    for odd in range(2):
+    tall = share // STEPS
+
+    def gather(odd):
+        mine[odd].wait()
         for r in range(shards):
 
             @pl.when(s != r)
             def _():
                 arrival(odd, r).wait_recv()
 
-    tall = share // STEPS
-
-    def gather(t, carry):
-        column, piece = t // STEPS, t % STEPS
-        for odd in range(2):
+        def piece(t, carry):
+            column, piece = t // STEPS, t % STEPS
             arrays = []
             for u in range(fan):
                 block = landed.at[odd, column * fan + u]
@@ -599,9 +601,12 @@
             for i, slope_part in enumerate(swap_lanes(arrays, width)):
                 at = pl.ds(2 * tall * piece + odd, tall, stride=2)
                 gathered[column, i // 2 % 2, i % 2, i // 4, at, :] = slope_part
-        return carry
-
-    lax.fori_loop(0, gathered.shape[0] * STEPS, gather, 0)
+            return carry
+
+        lax.fori_loop(0, gathered.shape[0] * STEPS, piece, 0)
+
+    for odd in range(2):
+        gather(odd)
     stores = [
         pltpu.make_async_copy(
             gathered.at[i],
@@ -703,8 +708,9 @@
     )(*inputs, raw, matrix, twiddle)
 
 
-def finish_kernel(width, fan, values, gate_in, gate_out, cotangent, found, *outs):
+def finish_kernel(width, fan, values, gate_in, gate_out, cotangent, found, slopes, *outs):
     rows = found.shape[2]
+    outs[4][...] = slopes[...]
     for block in range(found.shape[1] // fan):
         conv, back = (
             swap_lanes([found[sig, block * fan + u] for u in range(fan)], width)
@@ -723,22 +729,26 @@
             outs[3][here, lanes] = (wide(cotangent) * conv[g]).astype(jnp.bfloat16)
 
 
-def finish(inputs, found):
+def finish(inputs, found, slopes):
     rows, channels = inputs[0].shape
     _, devices, short, _ = found.shape
     width = channels // devices
     fan = LANES // width
-    tiles = channels // LANES // STEPS
+    steps = 2
+    tiles = channels // LANES // steps
     column = pl.BlockSpec((rows, tiles * LANES), lambda t: (0, t))
+    shape = slopes.shape
+    part = pl.BlockSpec(shape[:3] + (shape[3] // steps, shape[4]), lambda t: (0, 0, 0, t, 0))
     return pl.pallas_call(
         functools.partial(finish_kernel, width, fan),
-        grid=(STEPS,),
-        out_shape=tuple(jax.ShapeDtypeStruct((rows, channels), jnp.bfloat16) for _ in range(4)),
+        grid=(steps,),
+        out_shape=tuple(jax.ShapeDtypeStruct((rows, channels), jnp.bfloat16) for _ in range(4))
+        + (jax.ShapeDtypeStruct(shape, jnp.float32),),
         in_specs=[column] * 4
-        + [pl.BlockSpec((2, tiles * fan, short, LANES), lambda t: (0, t, 0, 0))],
-        out_specs=(column,) * 4,
+        + [pl.BlockSpec((2, tiles * fan, short, LANES), lambda t: (0, t, 0, 0)), part],
+        out_specs=(column,) * 4 + (part,),
         name="finish",
-    )(*inputs, found)
+    )(*inputs, found, slopes)
 
 
 def make_tables(shards, fan, length):
@@ -764,7 +774,8 @@
     fan = LANES * shards * groups // channels
     tables = make_tables(shards, fan, rows * groups // 2)
     found, slopes = convolve(inputs, filter_spectra, tables, shards, groups)
-    return tuple(finish(inputs, found)) + (slopes.reshape(filter_spectra.shape),)
+    outs = finish(inputs, found, slopes)
+    return tuple(outs[:4]) + (outs[4].reshape(filter_spectra.shape),)
 
 
 def solution(mesh):

time: 73.9 us -> 70.8 us (0.958)
  local copies, waits for them, and re-layouts: 1.33 us -> 0 us
  Pallas kernels: 70.5 us -> 69.2 us
    pallas_call x1, Pallas kernels: 66.3 us -> 64.9 us  [convolve(): pl.pallas_call(functools.partial(convolve_kernel, shards, groups), out_sh...]
    unnamed x3 -> x0, local copies, waits for them, and re-layouts: 1.33 us -> none
where the time goes in v5:
time: 70.8 us; the launch traced here: 69.8 us
  Pallas kernels  69.2 us (98%)
    pallas_call x1, Pallas kernels, convolve(): pl.pallas_call(functools.partial(convolve_kernel, shards, groups), out_sh...  64.9 us
    pallas_call x1, Pallas kernels, finish(): pl.pallas_call(functools.partial(finish_kernel, width, fan), grid=(steps,...  4.29 us

profile of v5, /device:TPU:0, one launch (start us, length us, event | category | flops | bytes accessed | tf_op | source)
XLA Modules:
  0.0 69.8 jit_solution(14749865385214109188)
XLA Ops:
  0.6 64.9 %convolve.1 = (f32[2,32,32,128]{3,2,1,0:T(8,128)}, f32[2,2,1,512,256]{4,3,2,1,0:T(8,128)}) custom-call(bf16[128,1024]{1,0:T(8,128)(2,1)} %values.1, bf16[128,1024]{1,0:T(8,128)(2,1)} %gate_in.1, bf16[128,1024]{1,0:T(8,128)(2,1)} %gate_out.1, bf16[128,1024]{1,0:T(8,128)(2,1)} %cotangent.1, f32[2,2,1,512,256]{4,3,2,1,0:T(8,128)} %bitcast.4, ...), custom_call_target="tpu_custom_call" | custom-call | tf_op jit(solution)/shard_map/convolve/pallas_call | solution.py:662
  65.5 4.3 %finish.1 = (bf16[128,1024]{1,0:T(8,128)(2,1)}, bf16[128,1024]{1,0:T(8,128)(2,1)}, bf16[128,1024]{1,0:T(8,128)(2,1)}, bf16[128,1024]{1,0:T(8,128)(2,1)}, f32[2,2,1,512,256]{4,3,2,1,0:T(8,128)}) custom-call(bf16[128,1024]{1,0:T(8,128)(2,1)} %values.1, bf16[128,1024]{1,0:T(8,128)(2,1)} %gate_in.1, bf16[128,1024]{1,0:T(8,128)(2,1)} %gate_out.1, ...), custom_call_target="tpu_custom_call" | custom-call | tf_op jit(solution)/shard_map/finish/pallas_call | solution.py:742

commit v6 on v5

--- a/solution.py
+++ b/solution.py
@@ -202,12 +202,14 @@
     couples = [list(range(n, min(n + 2, main + 1))) for n in range(0, main + 1, 2)]
 
     loads = [pltpu.make_async_copy(inputs[a], tokens.at[a], in_sem.at[a]) for a in range(4)]
-    loads.append(pltpu.make_async_copy(matrix_in, matrix, in_sem.at[4]))
-    loads.append(pltpu.make_async_copy(twiddle_in, twiddle, in_sem.at[5]))
+    tables_in = [
+        pltpu.make_async_copy(matrix_in, matrix, in_sem.at[4]),
+        pltpu.make_async_copy(twiddle_in, twiddle, in_sem.at[5]),
+    ]
     for i in range(raw.shape[0]):
         part = filt.at[:, :, :, :, pl.ds(i * LANES, LANES)]
         loads.append(pltpu.make_async_copy(part, raw.at[i], in_sem.at[6 + i]))
-    for load in loads:
+    for load in loads + tables_in:
         load.start()
 
     peers = [(j, d) for d in range(groups) for j in range(shards) if j or d]
@@ -298,8 +300,7 @@
     pl.semaphore_wait(barrier, len(peers))
     for j, d in peers:
         token(0, j, d, False).start()
-    arrange(1)
-    for load in loads[6:]:
+    for load in loads[4:]:
         load.wait()
     wide = raw.shape[4]
     span = wide // 2 // STEPS
@@ -331,6 +332,7 @@
     pending = list(range(1, shards))
     for j in pending:
         spectrum(j, False).start()
+    arrange(1)
     for j, d in peers:
         if j < 2:
             token(1, j, d, False).start()
@@ -363,8 +365,8 @@
     for j, d in peers:
         if j >= 2:
             token(1, j, d, False).start()
-    loads[4].wait()
-    loads[5].wait()
+    for load in tables_in:
+        load.wait()
 
     def zero():
         return jnp.zeros((step, LANES), jnp.float32)
@@ -449,9 +451,14 @@
                 result[sig, b // 2, (b % 2) * near + c1, here, :] = value
             return carry
 
-        lax.fori_loop(0, near * chunks, chunk, 0)
-        for j, d in peers:
-            outcome(sig, j, d, False).start()
+        for part in range(near):
+            lax.fori_loop(part * chunks, (part + 1) * chunks, chunk, 0)
+            for j, d in peers:
+
+                @pl.when((c ^ d) % near == part)
+                def _():
+                    outcome(sig, j, d, False).start()
+
 
     flip = (
         lax.broadcasted_iota(jnp.int32, (length, length), 0)

time: 70.8 us -> 70.2 us (level)
  no operation moved by 1% of the time
where the time goes in v6:
time: 70.2 us; the launch traced here: 69.8 us
  Pallas kernels  69.2 us (99%)
    pallas_call x1, Pallas kernels, convolve(): pl.pallas_call(functools.partial(convolve_kernel, shards, groups), out_sh...  64.9 us
    pallas_call x1, Pallas kernels, finish(): pl.pallas_call(functools.partial(finish_kernel, width, fan), grid=(steps,...  4.29 us

profile of v6, /device:TPU:0, one launch (start us, length us, event | category | flops | bytes accessed | tf_op | source)
XLA Modules:
  0.0 69.8 jit_solution(17573574682729847909)
XLA Ops:
  0.6 64.9 %convolve.1 = (f32[2,32,32,128]{3,2,1,0:T(8,128)}, f32[2,2,1,512,256]{4,3,2,1,0:T(8,128)}) custom-call(bf16[128,1024]{1,0:T(8,128)(2,1)} %values.1, bf16[128,1024]{1,0:T(8,128)(2,1)} %gate_in.1, bf16[128,1024]{1,0:T(8,128)(2,1)} %gate_out.1, bf16[128,1024]{1,0:T(8,128)(2,1)} %cotangent.1, f32[2,2,1,512,256]{4,3,2,1,0:T(8,128)} %bitcast.4, ...), custom_call_target="tpu_custom_call" | custom-call | tf_op jit(solution)/shard_map/convolve/pallas_call | solution.py:669
  65.5 4.3 %finish.1 = (bf16[128,1024]{1,0:T(8,128)(2,1)}, bf16[128,1024]{1,0:T(8,128)(2,1)}, bf16[128,1024]{1,0:T(8,128)(2,1)}, bf16[128,1024]{1,0:T(8,128)(2,1)}, f32[2,2,1,512,256]{4,3,2,1,0:T(8,128)}) custom-call(bf16[128,1024]{1,0:T(8,128)(2,1)} %values.1, bf16[128,1024]{1,0:T(8,128)(2,1)} %gate_in.1, bf16[128,1024]{1,0:T(8,128)(2,1)} %gate_out.1, ...), custom_call_target="tpu_custom_call" | custom-call | tf_op jit(solution)/shard_map/finish/pallas_call | solution.py:749
